TPU v7x, 32 devices: a whole 2x2x4 slice. The times are simulated.
32 devices in a mesh: groups: 2 (over x), wide: 8 (over z, y), narrow: 2 (over core).
Axes of the slice: x: 2, y: 2, z: 4, core: 2. Of those that a mesh axis runs over, the one named last changes fastest.
Arguments:
- tokens: bfloat16 [2048, 2048], P(('groups', 'wide', 'narrow')), parts along dimension 0, may hold values from -6 to 6
- gate_wts: bfloat16 [2048, 8], P(('groups', 'wide', 'narrow')), parts along dimension 0, may hold values from 0.099609375 to 1
- expert_ids: int32 [2048, 8], P(('groups', 'wide', 'narrow')), parts along dimension 0, may hold values from 0 to 23, as said below
- replica: int32 [2048, 8], P(('groups', 'wide', 'narrow')), parts along dimension 0, may hold values from 0 to 1, as said below
- w_gate: bfloat16 [32, 2048, 384], P(('wide', 'narrow')), may hold values from -0.125 to 0.125
- w_up: bfloat16 [32, 2048, 384], P(('wide', 'narrow')), may hold values from -0.125 to 0.125
- w_down: bfloat16 [32, 384, 2048], P(('wide', 'narrow')), may hold values from -0.3125 to 0.3125
- queries: bfloat16 [64, 32, 128], P(('groups', 'wide', 'narrow')), parts along dimension 0, may hold values from -80 to 80
- k_cache: bfloat16 [64, 640, 4, 128], P(('groups', 'wide', 'narrow')), parts along dimension 0, may hold values from -4 to 4
- value_cache: bfloat16 [64, 640, 4, 128], P(('groups', 'wide', 'narrow')), parts along dimension 0, may hold values from -5 to 5
- lengths: int32 [64], P(('groups', 'wide', 'narrow')), parts along dimension 0, may hold values from 80 to 640, as said below
Outputs:
- routed_out: bfloat16 [2048, 2048], P(('groups', 'wide', 'narrow')), parts along dimension 0
- attn_out: bfloat16 [64, 4096], P(('groups', 'wide', 'narrow')), parts along dimension 0
There are 2 independent parts, one for each index of `groups`. A program takes and returns all parts, laid end to end along the dimension named above; an argument that names none is the same for every part. Nothing has to cross between parts.
Inputs may be any that keep to these rules, and one draw needn't show every extreme that they name: `expert_ids`: each row names 8 different experts. Counted over the rows of one device (aligned blocks of 64 rows), the rows whose slots lie on one device number at most 64; one device, the same for every block of a draw, gets exactly 64 rows from every block. `replica`: 1 only where the named expert is below 8. `lengths`: one request of each draw has exactly 640 live positions.
All inputs are finite; a program needn't handle non-finite values.
Results may differ from a plain program's by a relative error of at most 0.008.
Values may be sent and summed in bfloat16 or wider, within the bound.
No kernel may reach another device: no remote copies, remote signals or barrier semaphores. Data moves between devices by JAX's collectives and lax.ppermute only.
A program may use at most 128 MiB of HBM per device.

v0:
```python
import functools

import jax
import jax.numpy as jnp
from jax import lax
from jax.experimental import pallas as pl
from jax.experimental.pallas import tpu as pltpu
from jax.sharding import PartitionSpec as P


SLOT_DEV = 2
LANES = 128
AXES = ("wide", "narrow")
VMEM_LIMIT = 24 << 20


def attend(queries, k_cache, value_cache, lengths):
    reqs, heads, head_dim = queries.shape
    kv_heads = k_cache.shape[2]
    group = heads // kv_heads
    grouped = queries.reshape(reqs, kv_heads, group, head_dim)
    scores = jnp.einsum(
        "rkgd,rlkd->rkgl", grouped, k_cache, preferred_element_type=jnp.float32
    ) * head_dim ** (-0.5)
    valid = jnp.arange(k_cache.shape[1], dtype=jnp.int32)[None, :] < lengths[:, None]
    valid = valid[:, None, None, :]
    scores = jnp.where(valid, scores, -1e30)
    top = jnp.max(scores, axis=-1, keepdims=True)
    expd = jnp.where(valid, jnp.exp(scores - top), 0.0)
    probs = (expd / jnp.sum(expd, axis=-1, keepdims=True)).astype(jnp.bfloat16)
    mixed = jnp.einsum("rkgl,rlkd->rkgd", probs, value_cache, preferred_element_type=jnp.float32)
    return mixed.astype(jnp.bfloat16).reshape(reqs, heads * head_dim)


def pack_kernel(experts, spares, tokens_ref, gate_ref, ids_ref, replica_ref, out_ref):
    rows, width = tokens_ref.shape
    extra = out_ref.shape[1] - width
    ids = ids_ref[...]
    slots = jnp.where((replica_ref[...] == 1) & (ids < spares), ids + experts, ids)
    weights = gate_ref[...].astype(jnp.float32)
    slot = lax.broadcasted_iota(jnp.int32, (extra, rows), 0)
    coef = jnp.zeros((extra, rows), jnp.float32)
    for k in range(ids.shape[0]):
        coef = coef + jnp.where(slot == slots[k : k + 1, :], weights[k : k + 1, :], 0.0)
    out_ref[:, :width] = tokens_ref[...]
    out_ref[:, width:] = coef.T.astype(out_ref.dtype)


def pack(tokens, gate_wts, expert_ids, replica, devices):
    rows, width = tokens.shape
    extra = pl.cdiv(SLOT_DEV * devices, LANES) * LANES
    return pl.pallas_call(
        functools.partial(pack_kernel, 3 * devices // 2, devices // 2),
        out_shape=jax.ShapeDtypeStruct((rows, width + extra), tokens.dtype),
        name="pack",
    )(tokens, gate_wts.T, expert_ids.T, replica.T)


def stage_kernel(first_ref, gate, up, down, gu_ref, down_ref, sem):
    slots, _, half = gate.shape
    copies = []
    for j in range(slots):
        copies.append(pltpu.make_async_copy(gate.at[j], gu_ref.at[j, :, pl.ds(0, half)], sem.at[j, 0]))
        copies.append(pltpu.make_async_copy(up.at[j], gu_ref.at[j, :, pl.ds(half, half)], sem.at[j, 1]))
        copies.append(pltpu.make_async_copy(down.at[j], down_ref.at[j], sem.at[j, 2]))
    for copy in copies:
        copy.start()
    for copy in copies:
        copy.wait()


def stage(first, gate, up, down):
    slots, width, half = gate.shape
    anywhere = pl.BlockSpec(memory_space=pl.ANY)
    return pl.pallas_call(
        stage_kernel,
        out_shape=[
            pltpu.VMEM((slots, width, 2 * half), gate.dtype),
            pltpu.VMEM((slots, half, width), down.dtype),
        ],
        in_specs=[pl.BlockSpec(memory_space=pltpu.SMEM)] + [anywhere] * 3,
        out_specs=[anywhere] * 2,
        scratch_shapes=[pltpu.SemaphoreType.DMA((slots, 3))],
        compiler_params=pltpu.CompilerParams(vmem_limit_bytes=4 << 20),
        name="stage",
    )(first, *(pltpu.with_memory_space_constraint(w, pltpu.HBM) for w in (gate, up, down)))


def expert_kernel(count, sources, base, with_sum, first_ref, *refs):
    blocks, refs = refs[:count], refs[count:]
    weights, refs = refs[: 2 * sources], refs[2 * sources :]
    sums, refs = (refs[:count], refs[count:]) if with_sum else ((), refs)
    outs, refs = refs[:count], refs[count:]
    x_ref, hidden_ref, x_sem = refs
    rows = blocks[0].shape[0]
    slots, half, width = weights[1].shape
    copies = [
        pltpu.make_async_copy(blocks[i], x_ref.at[pl.ds(i * rows, rows)], x_sem.at[i])
        for i in range(count)
    ]
    for copy in copies:
        copy.start()
    for copy in copies:
        copy.wait()
    shares = x_ref[:, width:].astype(jnp.float32)
    lane = lax.broadcasted_iota(jnp.int32, shares.shape, 1)
    result = None
    for n in range(sources):
        gu_ref, down_ref = weights[2 * n : 2 * n + 2]
        for j in range(slots):
            coef = jnp.sum(jnp.where(lane == first_ref[base + n] + j, shares, 0.0), axis=1, keepdims=True)
            both = jnp.dot(x_ref[:, :width], gu_ref[j], preferred_element_type=jnp.float32)
            gated, upward = both[:, :half], both[:, half:]
            hidden = gated / (1.0 + jnp.exp(-gated)) * upward * coef
            hidden_ref[:, j * half : (j + 1) * half] = hidden.astype(hidden_ref.dtype)
        down = down_ref[...].reshape(slots * half, width)
        part = jnp.dot(hidden_ref[...], down, preferred_element_type=jnp.float32)
        result = part if result is None else result + part
    for i in range(count):
        part = result[i * rows : (i + 1) * rows]
        if with_sum:
            part = part + sums[i][...]
        outs[i][...] = part.astype(outs[i].dtype)


def expert(blocks, weights, base, first, sums, dtype):
    count = len(blocks)
    sources = len(weights) // 2
    rows, packed = blocks[0].shape
    slots, half, width = weights[1].shape
    anywhere = pl.BlockSpec(memory_space=pl.ANY)
    whole = pl.BlockSpec(memory_space=pltpu.VMEM)
    weights = [pltpu.with_memory_space_constraint(w, pltpu.VMEM) for w in weights]
    return pl.pallas_call(
        functools.partial(expert_kernel, count, sources, base, bool(sums)),
        out_shape=[jax.ShapeDtypeStruct((rows, width), dtype)] * count,
        in_specs=[pl.BlockSpec(memory_space=pltpu.SMEM)]
        + [anywhere] * count
        + [whole] * (len(weights) + len(sums)),
        out_specs=[whole] * count,
        scratch_shapes=[
            pltpu.VMEM((count * rows, packed), blocks[0].dtype),
            pltpu.VMEM((count * rows, slots * half), blocks[0].dtype),
            pltpu.SemaphoreType.DMA((count,)),
        ],
        compiler_params=pltpu.CompilerParams(vmem_limit_bytes=VMEM_LIMIT),
        name="expert",
    )(first, *blocks, *weights, *sums)


def permutations(chips):
    ring = list(range(0, chips, 2)) + list(range(chips - 1 - chips % 2, 0, -2))
    step = {ring[i]: ring[(i + 1) % chips] for i in range(chips)}
    same = [(2 * a, 2 * b) for a, b in step.items()] + [(2 * b + 1, 2 * a + 1) for a, b in step.items()]
    cross = [(2 * a + 1, 2 * b) for a, b in step.items()] + [(2 * b, 2 * a + 1) for a, b in step.items()]
    return same, cross, [(b, a) for a, b in same], [(b, a) for a, b in cross]


def local(
    tokens,
    gate_wts,
    expert_ids,
    replica,
    w_gate,
    w_up,
    w_down,
    queries,
    k_cache,
    value_cache,
    lengths,
):
    chips = lax.axis_size("wide")
    devices = chips * lax.axis_size("narrow")
    same, cross, same_back, cross_back = permutations(chips)
    far = chips // 2
    core = lax.axis_index("narrow")
    me = lax.axis_index("wide") * 2 + core
    mine_first = me * SLOT_DEV
    theirs_first = (me + 1 - 2 * core) * SLOT_DEV
    first = jnp.stack([mine_first, theirs_first]).astype(jnp.int32)
    own = pack(tokens, gate_wts, expert_ids, replica, devices)
    near_rows, far_rows = {}, {}
    near_rows[1] = lax.ppermute(own, AXES, same)
    far_rows[1] = lax.ppermute(own, AXES, cross)
    swapped = []
    for w in (w_gate, w_up, w_down):
        swapped.append(lax.ppermute(w, "narrow", [(0, 1), (1, 0)]))
    mine = list(stage(first, w_gate, w_up, w_down))
    theirs = list(stage(first, *swapped))
    for k in range(2, far + 1):
        near_rows[k] = lax.ppermute(near_rows[k - 1], AXES, same)
        if k < far:
            far_rows[k] = lax.ppermute(far_rows[k - 1], AXES, same)
    partial = {}
    for group in groups_of(far):
        names, blocks = [], []
        for k in group:
            if k == 0:
                names.append(("own", 0))
                blocks.append(own)
                continue
            names.append(("near", k))
            blocks.append(near_rows[k])
            if k < far:
                names.append(("far", k))
                blocks.append(far_rows[k])
        top = group[-1]
        if top == far:
            outs = expert(blocks, mine + theirs, 0, first, [], jnp.bfloat16)
        else:
            sums = expert(blocks, mine, 0, first, [], jnp.float32)
            outs = expert(blocks, theirs, 1, first, sums, jnp.bfloat16)
        partial.update(zip(names, outs, strict=True))
    near_sum = partial["near", far]
    far_sum = partial["far", far - 1]
    for k in range(far - 1, 0, -1):
        near_sum = lax.ppermute(near_sum, AXES, same_back)
        near_sum = add(near_sum, partial["near", k])
        if k < far - 1:
            far_sum = lax.ppermute(far_sum, AXES, same_back)
            far_sum = add(far_sum, partial["far", k])
    near_sum = lax.ppermute(near_sum, AXES, same_back)
    far_sum = lax.ppermute(far_sum, AXES, cross_back)
    lengths, own_part = lax.optimization_barrier((lengths, partial["own", 0]))
    attn_out = attend(queries, k_cache, value_cache, lengths)
    routed_out = add(near_sum, far_sum, own_part)
    return (routed_out, attn_out)


def add(*values):
    return sum(v.astype(jnp.float32) for v in values).astype(jnp.bfloat16)


def groups_of(far):
    groups = []
    while far > 2:
        groups.append([far - 1, far])
        far -= 2
    groups.append(list(range(far + 1)))
    return groups[::-1]


def solution(mesh):
    rows = P(("groups", "wide", "narrow"))
    slots = P(("wide", "narrow"))
    in_specs = (rows, rows, rows, rows, slots, slots, slots, rows, rows, rows, rows)
    return jax.shard_map(local, mesh=mesh, in_specs=in_specs, out_specs=(rows, rows), check_vma=False)
```

profile of v0, /device:TPU:0, one launch (start us, length us, event | category | flops | bytes accessed | tf_op | source)
XLA Modules:
  0.0 77.2 jit_solution(5103944488731937849)
XLA Ops:
  0.6 0.0 copy-start
  0.6 0.6 collective-permute-start.7
  1.2 0.1 collective-permute-start.8
  1.3 0.4 collective-permute-start.9
  1.7 1.8 %pack.1.refs_0_ = bf16[64,2176]{1,0:T(8,128)(2,1)} custom-call(bf16[64,2048]{1,0:T(8,128)(2,1)} %tokens_ref.1, bf16[8,64]{1,0:T(8,128)(2,1)} %bitcast.19, s32[8,64]{1,0:T(8,128)} %bitcast.17, s32[8,64]{1,0:T(8,128)} %bitcast.18), custom_call_target="tpu_custom_call" | custom-call | tf_op jit(solution)/shard_map/pack/pallas_call | solution.py:52
  3.5 2.6 %collective-permute-start = (bf16[64,2176]{1,0:T(8,128)(2,1)}, bf16[64,2176]{1,0:T(8,128)(2,1)S(1)}, u32[]{:S(2)}, u32[]{:S(2)}) collective-permute-start(bf16[64,2176]{1,0:T(8,128)(2,1)} %pack.1.refs_0_), channel_id=1, source_target_pairs={{0,4},{4,8},{8,12},{12,14},{14,10},{10,6},{6,2},{2,0},{5,1},{9,5},... | collective-permute-start | bytes 835592 | tf_op jit(solution)/shard_map/ppermute | solution.py:183
  6.2 1.3 %collective-permute-start.3 = (bf16[64,2176]{1,0:T(8,128)(2,1)}, bf16[64,2176]{1,0:T(8,128)(2,1)S(1)}, u32[]{:S(2)}, u32[]{:S(2)}) collective-permute-start(bf16[64,2176]{1,0:T(8,128)(2,1)} %pack.1.refs_0_), channel_id=1, source_target_pairs={{1,4},{5,8},{9,12},{13,14},{15,10},{11,6},{7,2},{3,0},{4,1},{8,5},... | collective-permute-start | bytes 835592 | tf_op jit(solution)/shard_map/ppermute | solution.py:184
  7.4 5.1 %collective-permute-done.refs_1_ = bf16[64,2176]{1,0:T(8,128)(2,1)S(1)} collective-permute-done((bf16[64,2176]{1,0:T(8,128)(2,1)}, bf16[64,2176]{1,0:T(8,128)(2,1)S(1)}, u32[]{:S(2)}, u32[]{:S(2)}) %collective-permute-start) | collective-permute-done | bytes 278560 | tf_op jit(solution)/shard_map/ppermute | solution.py:183
  12.5 2.4 %collective-permute-start.1 = (bf16[64,2176]{1,0:T(8,128)(2,1)S(1)}, bf16[64,2176]{1,0:T(8,128)(2,1)S(1)}, u32[]{:S(2)}, u32[]{:S(2)}) collective-permute-start(bf16[64,2176]{1,0:T(8,128)(2,1)S(1)} %collective-permute-done.refs_1_), channel_id=1, source_target_pairs={{0,4},{4,8},{8,12},{12,14},{14,10},{10,6},{6,2},{2,0},{5,1},{9,5},... | collective-permute-start | bytes 835592 | tf_op jit(solution)/shard_map/ppermute | solution.py:191
  14.9 0.0 collective-permute-done.3.refs_2_
  14.9 1.6 %collective-permute-start.4 = (bf16[64,2176]{1,0:T(8,128)(2,1)S(1)}, bf16[64,2176]{1,0:T(8,128)(2,1)S(1)}, u32[]{:S(2)}, u32[]{:S(2)}) collective-permute-start(bf16[64,2176]{1,0:T(8,128)(2,1)S(1)} %collective-permute-done.3.refs_2_), channel_id=1, source_target_pairs={{0,4},{4,8},{8,12},{12,14},{14,10},{10,6},{6,2},{2,0},{5,1},{9,5},... | collective-permute-start | bytes 835592 | tf_op jit(solution)/shard_map/ppermute | solution.py:193
  16.5 3.3 %collective-permute-done.1.refs_3_ = bf16[64,2176]{1,0:T(8,128)(2,1)S(1)} collective-permute-done((bf16[64,2176]{1,0:T(8,128)(2,1)S(1)}, bf16[64,2176]{1,0:T(8,128)(2,1)S(1)}, u32[]{:S(2)}, u32[]{:S(2)}) %collective-permute-start.1) | collective-permute-done | bytes 278560 | tf_op jit(solution)/shard_map/ppermute | solution.py:191
  19.7 1.7 %collective-permute-start.2 = (bf16[64,2176]{1,0:T(8,128)(2,1)S(1)}, bf16[64,2176]{1,0:T(8,128)(2,1)S(1)}, u32[]{:S(2)}, u32[]{:S(2)}) collective-permute-start(bf16[64,2176]{1,0:T(8,128)(2,1)S(1)} %collective-permute-done.1.refs_3_), channel_id=1, source_target_pairs={{0,4},{4,8},{8,12},{12,14},{14,10},{10,6},{6,2},{2,0},{5,1},{9,5},... | collective-permute-start | bytes 835592 | tf_op jit(solution)/shard_map/ppermute | solution.py:191
  21.4 1.3 %collective-permute-done.4.refs_4_ = bf16[64,2176]{1,0:T(8,128)(2,1)S(1)} collective-permute-done((bf16[64,2176]{1,0:T(8,128)(2,1)S(1)}, bf16[64,2176]{1,0:T(8,128)(2,1)S(1)}, u32[]{:S(2)}, u32[]{:S(2)}) %collective-permute-start.4) | collective-permute-done | bytes 278560 | tf_op jit(solution)/shard_map/ppermute | solution.py:193
  22.7 1.7 %collective-permute-start.5 = (bf16[64,2176]{1,0:T(8,128)(2,1)S(1)}, bf16[64,2176]{1,0:T(8,128)(2,1)S(1)}, u32[]{:S(2)}, u32[]{:S(2)}) collective-permute-start(bf16[64,2176]{1,0:T(8,128)(2,1)S(1)} %collective-permute-done.4.refs_4_), channel_id=1, source_target_pairs={{0,4},{4,8},{8,12},{12,14},{14,10},{10,6},{6,2},{2,0},{5,1},{9,5},... | collective-permute-start | bytes 835592 | tf_op jit(solution)/shard_map/ppermute | solution.py:193
  24.4 1.9 %collective-permute-done.2.refs_0_ = bf16[64,2176]{1,0:T(8,128)(2,1)S(1)} collective-permute-done((bf16[64,2176]{1,0:T(8,128)(2,1)S(1)}, bf16[64,2176]{1,0:T(8,128)(2,1)S(1)}, u32[]{:S(2)}, u32[]{:S(2)}) %collective-permute-start.2) | collective-permute-done | bytes 278560 | tf_op jit(solution)/shard_map/ppermute | solution.py:191
  26.3 1.7 %collective-permute-start.6 = (bf16[64,2176]{1,0:T(8,128)(2,1)S(1)}, bf16[64,2176]{1,0:T(8,128)(2,1)S(1)}, u32[]{:S(2)}, u32[]{:S(2)}) collective-permute-start(bf16[64,2176]{1,0:T(8,128)(2,1)S(1)} %collective-permute-done.2.refs_0_), channel_id=1, source_target_pairs={{0,4},{4,8},{8,12},{12,14},{14,10},{10,6},{6,2},{2,0},{5,1},{9,5},... | collective-permute-start | bytes 835592 | tf_op jit(solution)/shard_map/ppermute | solution.py:191
  28.0 0.1 pad_add_fusion.first_ref
  28.1 4.3 %stage.2 = (bf16[2,2048,768]{2,1,0:T(8,128)(2,1)S(1)}, bf16[2,384,2048]{2,1,0:T(8,128)(2,1)S(1)}) custom-call(s32[2]{0:T(128)S(1)} %pad_add_fusion.first_ref, bf16[2,2048,384]{2,1,0:T(8,128)(2,1)} %gate.1, bf16[2,2048,384]{2,1,0:T(8,128)(2,1)} %up.1, bf16[2,384,2048]{2,1,0:T(8,128)(2,1)} %down.1), custom_call_target="tpu_custom_call" | custom-call | tf_op jit(solution)/shard_map/stage/pallas_call | solution.py:75
  32.4 0.0 copy-done.1
  32.4 4.0 %expert.4 = (f32[64,2048]{1,0:T(8,128)S(1)}, f32[64,2048]{1,0:T(8,128)S(1)}, f32[64,2048]{1,0:T(8,128)S(1)}, f32[64,2048]{1,0:T(8,128)S(1)}, f32[64,2048]{1,0:T(8,128)S(1)}) custom-call(s32[2]{0:T(128)S(1)} %pad_add_fusion.first_ref, bf16[64,2176]{1,0:T(8,128)(2,1)S(1)} %copy-done.1, bf16[64,2176]{1,0:T(8,128)(2,1)S(1)} %collective-permute-done.refs_1_, ...), custom_call_target="tpu_custom_call" | custom-call | tf_op jit(solution)/shard_map/expert/pallas_call | solution.py:134
  36.4 0.0 collective-permute-done.7.gate
  36.4 0.0 collective-permute-done.8.up
  36.5 0.0 collective-permute-done.9.down
  36.5 4.3 %stage.3 = (bf16[2,2048,768]{2,1,0:T(8,128)(2,1)S(1)}, bf16[2,384,2048]{2,1,0:T(8,128)(2,1)S(1)}) custom-call(s32[2]{0:T(128)S(1)} %pad_add_fusion.first_ref, bf16[2,2048,384]{2,1,0:T(8,128)(2,1)} %collective-permute-done.7.gate, bf16[2,2048,384]{2,1,0:T(8,128)(2,1)} %collective-permute-done.8.up, bf16[2,384,2048]{2,1,0:T(8,128)(2,1)} %collective-permute-done.9.down), custom_call_target="tpu_custom_call" | custom-call | tf_op jit(solution)/shard_map/stage/pallas_call | solution.py:75
  40.8 4.0 %expert.5 = (bf16[64,2048]{1,0:T(8,128)(2,1)S(1)}, bf16[64,2048]{1,0:T(8,128)(2,1)S(1)}, bf16[64,2048]{1,0:T(8,128)(2,1)S(1)}, bf16[64,2048]{1,0:T(8,128)(2,1)S(1)}, bf16[64,2048]{1,0:T(8,128)(2,1)S(1)}) custom-call(s32[2]{0:T(128)S(1)} %pad_add_fusion.first_ref, bf16[64,2176]{1,0:T(8,128)(2,1)S(1)} %copy-done.1, ...), custom_call_target="tpu_custom_call" | custom-call | tf_op jit(solution)/shard_map/expert/pallas_call | solution.py:134
  44.8 0.0 copy-start.2
  44.9 0.0 copy-start.4
  44.9 0.0 copy-start.6
  44.9 0.0 copy-start.8
  44.9 0.0 copy-start.10
  44.9 0.0 copy-start.12
  44.9 0.0 collective-permute-done.5.refs_1_
  44.9 0.0 collective-permute-done.6.refs_2_
  44.9 5.3 %expert.3 = (bf16[64,2048]{1,0:T(8,128)(2,1)S(1)}, bf16[64,2048]{1,0:T(8,128)(2,1)S(1)}, bf16[64,2048]{1,0:T(8,128)(2,1)}) custom-call(s32[2]{0:T(128)S(1)} %pad_add_fusion.first_ref, bf16[64,2176]{1,0:T(8,128)(2,1)S(1)} %collective-permute-done.2.refs_0_, bf16[64,2176]{1,0:T(8,128)(2,1)S(1)} %collective-permute-done.5.refs_1_, ...), custom_call_target="tpu_custom_call" | custom-call | tf_op jit(solution)/shard_map/expert/pallas_call | solution.py:134
  50.2 0.0 copy-done.2
  50.2 0.0 copy-done.4
  50.3 0.0 copy-done.6
  50.3 0.4 collective-permute-start.10
  50.7 0.1 iota_compare_fusion
  50.7 2.0 %collective-permute-start.14 = (bf16[64,2048]{1,0:T(8,128)(2,1)S(1)}, bf16[64,2048]{1,0:T(8,128)(2,1)S(1)}, u32[]{:S(2)}, u32[]{:S(2)}) collective-permute-start(bf16[64,2048]{1,0:T(8,128)(2,1)S(1)} %get-tuple-element.34), channel_id=1, source_target_pairs={{4,0},{8,4},{12,8},{14,12},{10,14},{6,10},{2,6},{0,2},{1,5},{5,9},... | collective-permute-start | bytes 786440 | tf_op jit(solution)/shard_map/ppermute | solution.py:220
  52.8 1.3 %fusion.22 = (f32[2,4,8]{2,1,0:T(4,128)S(1)}, f32[2,4,8,640]{3,2,1,0:T(8,128)}) fusion(pred[2,640]{1,0:T(4,128)(4,1)S(1)} %iota_compare_fusion, bf16[2,640,4,128]{3,2,1,0:T(4,128)(2,1)S(1)} %copy-done, bf16[2,32,128]{2,1,0:T(8,128)(2,1)S(1)} %copy-done.12), kind=kOutput, calls=%fused_computation.24 | convolution fusion | flops 10691199 | bytes 1492480 | tf_op jit(solution)/shard_map/sub | solution.py:29
  54.1 2.9 %collective-permute-done.10 = bf16[64,2048]{1,0:T(8,128)(2,1)S(1)} collective-permute-done((bf16[64,2048]{1,0:T(8,128)(2,1)}, bf16[64,2048]{1,0:T(8,128)(2,1)S(1)}, u32[]{:S(2)}, u32[]{:S(2)}) %collective-permute-start.10) | collective-permute-done | bytes 262176 | tf_op jit(solution)/shard_map/ppermute | solution.py:217
  56.9 0.1 add_convert_fusion.5
  57.0 0.4 collective-permute-start.11
  57.4 2.4 %collective-permute-done.14 = bf16[64,2048]{1,0:T(8,128)(2,1)S(1)} collective-permute-done((bf16[64,2048]{1,0:T(8,128)(2,1)S(1)}, bf16[64,2048]{1,0:T(8,128)(2,1)S(1)}, u32[]{:S(2)}, u32[]{:S(2)}) %collective-permute-start.14) | collective-permute-done | bytes 262176 | tf_op jit(solution)/shard_map/ppermute | solution.py:220
  59.7 0.1 add_convert_fusion.2
  59.8 0.0 copy-start.11
  59.8 0.4 collective-permute-start.15
  60.2 3.2 %collective-permute-done.11 = bf16[64,2048]{1,0:T(8,128)(2,1)S(1)} collective-permute-done((bf16[64,2048]{1,0:T(8,128)(2,1)S(1)}, bf16[64,2048]{1,0:T(8,128)(2,1)S(1)}, u32[]{:S(2)}, u32[]{:S(2)}) %collective-permute-start.11) | collective-permute-done | bytes 262176 | tf_op jit(solution)/shard_map/ppermute | solution.py:217
  63.4 0.1 add_convert_fusion.4
  63.5 0.4 collective-permute-start.12
  63.9 2.4 %collective-permute-done.15 = bf16[64,2048]{1,0:T(8,128)(2,1)S(1)} collective-permute-done((bf16[64,2048]{1,0:T(8,128)(2,1)S(1)}, bf16[64,2048]{1,0:T(8,128)(2,1)S(1)}, u32[]{:S(2)}, u32[]{:S(2)}) %collective-permute-start.15) | collective-permute-done | bytes 262176 | tf_op jit(solution)/shard_map/ppermute | solution.py:220
  66.3 0.0 copy-done.3
  66.3 0.1 add_convert_fusion.1
  66.3 0.1 collective-permute-start.16
  66.4 3.5 %collective-permute-done.12 = bf16[64,2048]{1,0:T(8,128)(2,1)S(1)} collective-permute-done((bf16[64,2048]{1,0:T(8,128)(2,1)S(1)}, bf16[64,2048]{1,0:T(8,128)(2,1)S(1)}, u32[]{:S(2)}, u32[]{:S(2)}) %collective-permute-start.12) | collective-permute-done | bytes 262176 | tf_op jit(solution)/shard_map/ppermute | solution.py:217
  69.9 0.1 add_convert_fusion.3
  70.0 0.4 collective-permute-start.13
  70.4 0.4 fusion.17
  70.7 0.6 copy.31
  71.4 0.8 %collective-permute-done.16 = bf16[64,2048]{1,0:T(8,128)(2,1)S(1)} collective-permute-done((bf16[64,2048]{1,0:T(8,128)(2,1)S(1)}, bf16[64,2048]{1,0:T(8,128)(2,1)S(1)}, u32[]{:S(2)}, u32[]{:S(2)}) %collective-permute-start.16) | collective-permute-done | bytes 262176 | tf_op jit(solution)/shard_map/ppermute | solution.py:223
  72.2 4.2 %collective-permute-done.13 = bf16[64,2048]{1,0:T(8,128)(2,1)S(1)} collective-permute-done((bf16[64,2048]{1,0:T(8,128)(2,1)S(1)}, bf16[64,2048]{1,0:T(8,128)(2,1)S(1)}, u32[]{:S(2)}, u32[]{:S(2)}) %collective-permute-start.13) | collective-permute-done | bytes 262176 | tf_op jit(solution)/shard_map/ppermute | solution.py:222
  76.4 0.8 %add_convert_fusion = bf16[64,2048]{1,0:T(8,128)(2,1)} fusion(bf16[64,2048]{1,0:T(8,128)(2,1)S(1)} %copy-done.9, bf16[64,2048]{1,0:T(8,128)(2,1)S(1)} %collective-permute-done.16, bf16[64,2048]{1,0:T(8,128)(2,1)S(1)} %collective-permute-done.13), kind=kLoop, calls=%fused_computation.12 | loop fusion | flops 786432 | bytes 1048576 | tf_op jit(solution)/shard_map/convert_element_type | solution.py:231
  (15 shorter events, 0.0 us)
Async XLA Ops:
  0.6 52.1 %copy-start = (bf16[2,640,4,128]{3,2,1,0:T(4,128)(2,1)S(1)}, bf16[2,640,4,128]{3,2,1,0:T(4,128)(2,1)}, u32[]{:S(2)}) copy-start(bf16[2,640,4,128]{3,2,1,0:T(4,128)(2,1)} %param.19) | copy-start | bytes 3932164
  0.6 35.8 %collective-permute-start.7 = (bf16[2,2048,384]{2,1,0:T(8,128)(2,1)}, bf16[2,2048,384]{2,1,0:T(8,128)(2,1)}, u32[]{:S(2)}, u32[]{:S(2)}) collective-permute-start(bf16[2,2048,384]{2,1,0:T(8,128)(2,1)} %gate.1), channel_id=1, source_target_pairs={{0,1},{1,0},{2,3},{3,2},{4,5},{5,4},{6,7},{7,6},{8,9},{9,8},{10,11... | collective-permute-start | bytes 9437192 | tf_op jit(solution)/shard_map/ppermute | solution.py:187
  1.2 35.2 %collective-permute-start.8 = (bf16[2,2048,384]{2,1,0:T(8,128)(2,1)}, bf16[2,2048,384]{2,1,0:T(8,128)(2,1)}, u32[]{:S(2)}, u32[]{:S(2)}) collective-permute-start(bf16[2,2048,384]{2,1,0:T(8,128)(2,1)} %up.1), channel_id=1, source_target_pairs={{0,1},{1,0},{2,3},{3,2},{4,5},{5,4},{6,7},{7,6},{8,9},{9,8},{10,11... | collective-permute-start | bytes 9437192 | tf_op jit(solution)/shard_map/ppermute | solution.py:187
  1.3 35.2 %collective-permute-start.9 = (bf16[2,384,2048]{2,1,0:T(8,128)(2,1)}, bf16[2,384,2048]{2,1,0:T(8,128)(2,1)}, u32[]{:S(2)}, u32[]{:S(2)}) collective-permute-start(bf16[2,384,2048]{2,1,0:T(8,128)(2,1)} %down.1), channel_id=1, source_target_pairs={{0,1},{1,0},{2,3},{3,2},{4,5},{5,4},{6,7},{7,6},{8,9},{9,8},{10,11... | collective-permute-start | bytes 9437192 | tf_op jit(solution)/shard_map/ppermute | solution.py:187
  3.5 9.0 %collective-permute-start = (bf16[64,2176]{1,0:T(8,128)(2,1)}, bf16[64,2176]{1,0:T(8,128)(2,1)S(1)}, u32[]{:S(2)}, u32[]{:S(2)}) collective-permute-start(bf16[64,2176]{1,0:T(8,128)(2,1)} %pack.1.refs_0_), channel_id=1, source_target_pairs={{0,4},{4,8},{8,12},{12,14},{14,10},{10,6},{6,2},{2,0},{5,1},{9,5},... | collective-permute-start | bytes 835592 | tf_op jit(solution)/shard_map/ppermute | solution.py:183
  6.2 8.7 %collective-permute-start.3 = (bf16[64,2176]{1,0:T(8,128)(2,1)}, bf16[64,2176]{1,0:T(8,128)(2,1)S(1)}, u32[]{:S(2)}, u32[]{:S(2)}) collective-permute-start(bf16[64,2176]{1,0:T(8,128)(2,1)} %pack.1.refs_0_), channel_id=1, source_target_pairs={{1,4},{5,8},{9,12},{13,14},{15,10},{11,6},{7,2},{3,0},{4,1},{8,5},... | collective-permute-start | bytes 835592 | tf_op jit(solution)/shard_map/ppermute | solution.py:184
  12.5 7.2 %collective-permute-start.1 = (bf16[64,2176]{1,0:T(8,128)(2,1)S(1)}, bf16[64,2176]{1,0:T(8,128)(2,1)S(1)}, u32[]{:S(2)}, u32[]{:S(2)}) collective-permute-start(bf16[64,2176]{1,0:T(8,128)(2,1)S(1)} %collective-permute-done.refs_1_), channel_id=1, source_target_pairs={{0,4},{4,8},{8,12},{12,14},{14,10},{10,6},{6,2},{2,0},{5,1},{9,5},... | collective-permute-start | bytes 835592 | tf_op jit(solution)/shard_map/ppermute | solution.py:191
  14.9 7.8 %collective-permute-start.4 = (bf16[64,2176]{1,0:T(8,128)(2,1)S(1)}, bf16[64,2176]{1,0:T(8,128)(2,1)S(1)}, u32[]{:S(2)}, u32[]{:S(2)}) collective-permute-start(bf16[64,2176]{1,0:T(8,128)(2,1)S(1)} %collective-permute-done.3.refs_2_), channel_id=1, source_target_pairs={{0,4},{4,8},{8,12},{12,14},{14,10},{10,6},{6,2},{2,0},{5,1},{9,5},... | collective-permute-start | bytes 835592 | tf_op jit(solution)/shard_map/ppermute | solution.py:193
  19.7 6.5 %collective-permute-start.2 = (bf16[64,2176]{1,0:T(8,128)(2,1)S(1)}, bf16[64,2176]{1,0:T(8,128)(2,1)S(1)}, u32[]{:S(2)}, u32[]{:S(2)}) collective-permute-start(bf16[64,2176]{1,0:T(8,128)(2,1)S(1)} %collective-permute-done.1.refs_3_), channel_id=1, source_target_pairs={{0,4},{4,8},{8,12},{12,14},{14,10},{10,6},{6,2},{2,0},{5,1},{9,5},... | collective-permute-start | bytes 835592 | tf_op jit(solution)/shard_map/ppermute | solution.py:191
  22.7 22.2 %collective-permute-start.5 = (bf16[64,2176]{1,0:T(8,128)(2,1)S(1)}, bf16[64,2176]{1,0:T(8,128)(2,1)S(1)}, u32[]{:S(2)}, u32[]{:S(2)}) collective-permute-start(bf16[64,2176]{1,0:T(8,128)(2,1)S(1)} %collective-permute-done.4.refs_4_), channel_id=1, source_target_pairs={{0,4},{4,8},{8,12},{12,14},{14,10},{10,6},{6,2},{2,0},{5,1},{9,5},... | collective-permute-start | bytes 835592 | tf_op jit(solution)/shard_map/ppermute | solution.py:193
  26.3 18.6 %collective-permute-start.6 = (bf16[64,2176]{1,0:T(8,128)(2,1)S(1)}, bf16[64,2176]{1,0:T(8,128)(2,1)S(1)}, u32[]{:S(2)}, u32[]{:S(2)}) collective-permute-start(bf16[64,2176]{1,0:T(8,128)(2,1)S(1)} %collective-permute-done.2.refs_0_), channel_id=1, source_target_pairs={{0,4},{4,8},{8,12},{12,14},{14,10},{10,6},{6,2},{2,0},{5,1},{9,5},... | collective-permute-start | bytes 835592 | tf_op jit(solution)/shard_map/ppermute | solution.py:191
  28.1 4.3 %copy-start.1 = (bf16[64,2176]{1,0:T(8,128)(2,1)S(1)}, bf16[64,2176]{1,0:T(8,128)(2,1)}, u32[]{:S(2)}) copy-start(bf16[64,2176]{1,0:T(8,128)(2,1)} %pack.1.refs_0_) | copy-start | bytes 835588
  44.8 5.4 %copy-start.2 = (bf16[64,2048]{1,0:T(8,128)(2,1)}, bf16[64,2048]{1,0:T(8,128)(2,1)S(1)}, u32[]{:S(2)}) copy-start(bf16[64,2048]{1,0:T(8,128)(2,1)S(1)} %get-tuple-element.36) | copy-start | bytes 786436
  44.9 5.4 %copy-start.4 = (bf16[64,2048]{1,0:T(8,128)(2,1)}, bf16[64,2048]{1,0:T(8,128)(2,1)S(1)}, u32[]{:S(2)}) copy-start(bf16[64,2048]{1,0:T(8,128)(2,1)S(1)} %get-tuple-element.32) | copy-start | bytes 786436
  44.9 5.4 %copy-start.6 = (bf16[64,2048]{1,0:T(8,128)(2,1)}, bf16[64,2048]{1,0:T(8,128)(2,1)S(1)}, u32[]{:S(2)}) copy-start(bf16[64,2048]{1,0:T(8,128)(2,1)S(1)} %get-tuple-element.35) | copy-start | bytes 786436
  44.9 5.4 %copy-start.8 = (bf16[64,2048]{1,0:T(8,128)(2,1)}, bf16[64,2048]{1,0:T(8,128)(2,1)S(1)}, u32[]{:S(2)}) copy-start(bf16[64,2048]{1,0:T(8,128)(2,1)S(1)} %get-tuple-element.38) | copy-start | bytes 786436
  44.9 5.8 %copy-start.10 = (s32[2]{0:T(128)S(1)}, s32[2]{0:T(128)}, u32[]{:S(2)}) copy-start(s32[2]{0:T(128)} %param.21) | copy-start | bytes 28
  44.9 7.9 %copy-start.12 = (bf16[2,32,128]{2,1,0:T(8,128)(2,1)S(1)}, bf16[2,32,128]{2,1,0:T(8,128)(2,1)}, u32[]{:S(2)}) copy-start(bf16[2,32,128]{2,1,0:T(8,128)(2,1)} %param.18) | copy-start | bytes 49156
  50.3 9.5 %copy-start.7 = (bf16[64,2048]{1,0:T(8,128)(2,1)S(1)}, bf16[64,2048]{1,0:T(8,128)(2,1)}, u32[]{:S(2)}) copy-start(bf16[64,2048]{1,0:T(8,128)(2,1)} %copy-done.6) | copy-start | bytes 786436
  50.3 6.6 %collective-permute-start.10 = (bf16[64,2048]{1,0:T(8,128)(2,1)}, bf16[64,2048]{1,0:T(8,128)(2,1)S(1)}, u32[]{:S(2)}, u32[]{:S(2)}) collective-permute-start(bf16[64,2048]{1,0:T(8,128)(2,1)} %get-tuple-element.25), channel_id=1, source_target_pairs={{4,0},{8,4},{12,8},{14,12},{10,14},{6,10},{2,6},{0,2},{1,5},{5,9},... | collective-permute-start | bytes 786440 | tf_op jit(solution)/shard_map/ppermute | solution.py:217
  50.7 12.7 %copy-start.5 = (bf16[64,2048]{1,0:T(8,128)(2,1)S(1)}, bf16[64,2048]{1,0:T(8,128)(2,1)}, u32[]{:S(2)}) copy-start(bf16[64,2048]{1,0:T(8,128)(2,1)} %copy-done.4) | copy-start | bytes 786436
  50.7 9.0 %collective-permute-start.14 = (bf16[64,2048]{1,0:T(8,128)(2,1)S(1)}, bf16[64,2048]{1,0:T(8,128)(2,1)S(1)}, u32[]{:S(2)}, u32[]{:S(2)}) collective-permute-start(bf16[64,2048]{1,0:T(8,128)(2,1)S(1)} %get-tuple-element.34), channel_id=1, source_target_pairs={{4,0},{8,4},{12,8},{14,12},{10,14},{6,10},{2,6},{0,2},{1,5},{5,9},... | collective-permute-start | bytes 786440 | tf_op jit(solution)/shard_map/ppermute | solution.py:220
  54.1 12.2 %copy-start.3 = (bf16[64,2048]{1,0:T(8,128)(2,1)S(1)}, bf16[64,2048]{1,0:T(8,128)(2,1)}, u32[]{:S(2)}) copy-start(bf16[64,2048]{1,0:T(8,128)(2,1)} %copy-done.2) | copy-start | bytes 786436
  57.0 6.4 %collective-permute-start.11 = (bf16[64,2048]{1,0:T(8,128)(2,1)S(1)}, bf16[64,2048]{1,0:T(8,128)(2,1)S(1)}, u32[]{:S(2)}, u32[]{:S(2)}) collective-permute-start(bf16[64,2048]{1,0:T(8,128)(2,1)S(1)} %add_convert_fusion.5), channel_id=1, source_target_pairs={{4,0},{8,4},{12,8},{14,12},{10,14},{6,10},{2,6},{0,2},{1,5},{5,9},... | collective-permute-start | bytes 786440 | tf_op jit(solution)/shard_map/ppermute | solution.py:217
  59.8 10.6 %copy-start.11 = (bf16[2,640,4,128]{3,2,1,0:T(4,128)(2,1)S(1)}, bf16[2,640,4,128]{3,2,1,0:T(4,128)(2,1)}, u32[]{:S(2)}) copy-start(bf16[2,640,4,128]{3,2,1,0:T(4,128)(2,1)} %param.20) | copy-start | bytes 3932164
  59.8 10.5 %copy-start.13 = (f32[2,4,8,640]{3,2,1,0:T(8,128)S(1)}, f32[2,4,8,640]{3,2,1,0:T(8,128)}, u32[]{:S(2)}) copy-start(f32[2,4,8,640]{3,2,1,0:T(8,128)} %get-tuple-element.41) | copy-start | bytes 491524
  59.8 6.4 %collective-permute-start.15 = (bf16[64,2048]{1,0:T(8,128)(2,1)S(1)}, bf16[64,2048]{1,0:T(8,128)(2,1)S(1)}, u32[]{:S(2)}, u32[]{:S(2)}) collective-permute-start(bf16[64,2048]{1,0:T(8,128)(2,1)S(1)} %add_convert_fusion.2), channel_id=1, source_target_pairs={{4,0},{8,4},{12,8},{14,12},{10,14},{6,10},{2,6},{0,2},{1,5},{5,9},... | collective-permute-start | bytes 786440 | tf_op jit(solution)/shard_map/ppermute | solution.py:220
  63.5 6.4 %collective-permute-start.12 = (bf16[64,2048]{1,0:T(8,128)(2,1)S(1)}, bf16[64,2048]{1,0:T(8,128)(2,1)S(1)}, u32[]{:S(2)}, u32[]{:S(2)}) collective-permute-start(bf16[64,2048]{1,0:T(8,128)(2,1)S(1)} %add_convert_fusion.4), channel_id=1, source_target_pairs={{4,0},{8,4},{12,8},{14,12},{10,14},{6,10},{2,6},{0,2},{1,5},{5,9},... | collective-permute-start | bytes 786440 | tf_op jit(solution)/shard_map/ppermute | solution.py:217
  66.3 5.9 %collective-permute-start.16 = (bf16[64,2048]{1,0:T(8,128)(2,1)S(1)}, bf16[64,2048]{1,0:T(8,128)(2,1)S(1)}, u32[]{:S(2)}, u32[]{:S(2)}) collective-permute-start(bf16[64,2048]{1,0:T(8,128)(2,1)S(1)} %add_convert_fusion.1), channel_id=1, source_target_pairs={{4,1},{8,5},{12,9},{14,13},{10,15},{6,11},{2,7},{0,3},{1,4},{5,8},... | collective-permute-start | bytes 786440 | tf_op jit(solution)/shard_map/ppermute | solution.py:223
  69.9 6.5 %copy-start.9 = (bf16[64,2048]{1,0:T(8,128)(2,1)S(1)}, bf16[64,2048]{1,0:T(8,128)(2,1)}, u32[]{:S(2)}) copy-start(bf16[64,2048]{1,0:T(8,128)(2,1)} %copy-done.8) | copy-start | bytes 786436
  70.0 6.4 %collective-permute-start.13 = (bf16[64,2048]{1,0:T(8,128)(2,1)S(1)}, bf16[64,2048]{1,0:T(8,128)(2,1)S(1)}, u32[]{:S(2)}, u32[]{:S(2)}) collective-permute-start(bf16[64,2048]{1,0:T(8,128)(2,1)S(1)} %add_convert_fusion.3), channel_id=1, source_target_pairs={{4,0},{8,4},{12,8},{14,12},{10,14},{6,10},{2,6},{0,2},{1,5},{5,9},... | collective-permute-start | bytes 786440 | tf_op jit(solution)/shard_map/ppermute | solution.py:222
where the time goes:
time: 77.4 us; the launch traced here: 77.2 us
  waiting for transfers between devices  30.9 us (40%)
  Pallas kernels  23.8 us (31%)
  starting transfers between devices  18 us (23%)
  matrix products  1.64 us (2%)
  other arithmetic  1.28 us (2%)
  between operations  0.88 us (1%)
    ppermute x4, waiting for transfers between devices, local(): near_sum = lax.ppermute(near_sum, AXES, same_back)  13.8 us
    pallas_call x3, Pallas kernels, expert(): pl.pallas_call(functools.partial(expert_kernel, count, sources, base, boo...  13.3 us
    pallas_call x2, Pallas kernels, stage(): pl.pallas_call(stage_kernel, out_shape=[pltpu.VMEM((slots, width, 2 * hal...  8.66 us
    ppermute x3, starting transfers between devices, local(): near_rows[k] = lax.ppermute(near_rows[k - 1], AXES, same)  5.78 us
    ppermute x3, waiting for transfers between devices, local(): near_rows[k] = lax.ppermute(near_rows[k - 1], AXES, same)  5.13 us
    ppermute x1, waiting for transfers between devices, local(): near_rows[1] = lax.ppermute(own, AXES, same)  5.09 us
    ppermute x2, waiting for transfers between devices, local(): far_sum = lax.ppermute(far_sum, AXES, same_back)  4.75 us
    ppermute x2, starting transfers between devices, local(): far_rows[k] = lax.ppermute(far_rows[k - 1], AXES, same)  3.28 us
  transfers between devices with their start and end apart: 17, of which 11 were waited for; matrix products, arithmetic and copies ran while one was open for 4% of the time, Pallas kernels for 24%

commit v1 on v0

--- a/solution.py
+++ b/solution.py
@@ -32,28 +32,49 @@
     return mixed.astype(jnp.bfloat16).reshape(reqs, heads * head_dim)
 
 
-def pack_kernel(experts, spares, tokens_ref, gate_ref, ids_ref, replica_ref, out_ref):
-    rows, width = tokens_ref.shape
+def pack_kernel(experts, spares, tokens, gate, ids, replica, out_ref, gate_ref, ids_ref, replica_ref, sem):
+    rows, width = tokens.shape
     extra = out_ref.shape[1] - width
-    ids = ids_ref[...]
-    slots = jnp.where((replica_ref[...] == 1) & (ids < spares), ids + experts, ids)
+    copies = [
+        pltpu.make_async_copy(gate, gate_ref, sem.at[0]),
+        pltpu.make_async_copy(ids, ids_ref, sem.at[1]),
+        pltpu.make_async_copy(replica, replica_ref, sem.at[2]),
+        pltpu.make_async_copy(tokens, out_ref.at[:, pl.ds(0, width)], sem.at[3]),
+    ]
+    for copy in copies:
+        copy.start()
+    for copy in copies[:3]:
+        copy.wait()
+    slots = jnp.where(
+        (replica_ref[...] == 1) & (ids_ref[...] < spares), ids_ref[...] + experts, ids_ref[...]
+    )
     weights = gate_ref[...].astype(jnp.float32)
     slot = lax.broadcasted_iota(jnp.int32, (extra, rows), 0)
     coef = jnp.zeros((extra, rows), jnp.float32)
-    for k in range(ids.shape[0]):
+    for k in range(slots.shape[0]):
         coef = coef + jnp.where(slot == slots[k : k + 1, :], weights[k : k + 1, :], 0.0)
-    out_ref[:, :width] = tokens_ref[...]
     out_ref[:, width:] = coef.T.astype(out_ref.dtype)
+    copies[3].wait()
 
 
 def pack(tokens, gate_wts, expert_ids, replica, devices):
     rows, width = tokens.shape
+    top_count = gate_wts.shape[1]
     extra = pl.cdiv(SLOT_DEV * devices, LANES) * LANES
     return pl.pallas_call(
         functools.partial(pack_kernel, 3 * devices // 2, devices // 2),
         out_shape=jax.ShapeDtypeStruct((rows, width + extra), tokens.dtype),
+        in_specs=[pl.BlockSpec(memory_space=pl.ANY)] * 4,
+        out_specs=pl.BlockSpec(memory_space=pltpu.VMEM),
+        scratch_shapes=[
+            pltpu.VMEM((top_count, rows), gate_wts.dtype),
+            pltpu.VMEM((top_count, rows), expert_ids.dtype),
+            pltpu.VMEM((top_count, rows), replica.dtype),
+            pltpu.SemaphoreType.DMA((4,)),
+        ],
+        compiler_params=pltpu.CompilerParams(vmem_limit_bytes=4 << 20),
         name="pack",
-    )(tokens, gate_wts.T, expert_ids.T, replica.T)
+    )(*(pltpu.with_memory_space_constraint(v, pltpu.HBM) for v in (tokens, gate_wts.T, expert_ids.T, replica.T)))
 
 
 def stage_kernel(first_ref, gate, up, down, gu_ref, down_ref, sem):
@@ -182,11 +203,10 @@
     near_rows, far_rows = {}, {}
     near_rows[1] = lax.ppermute(own, AXES, same)
     far_rows[1] = lax.ppermute(own, AXES, cross)
-    swapped = []
-    for w in (w_gate, w_up, w_down):
-        swapped.append(lax.ppermute(w, "narrow", [(0, 1), (1, 0)]))
     mine = list(stage(first, w_gate, w_up, w_down))
-    theirs = list(stage(first, *swapped))
+    theirs = []
+    for w in mine:
+        theirs.append(lax.ppermute(w, "narrow", [(0, 1), (1, 0)]))
     for k in range(2, far + 1):
         near_rows[k] = lax.ppermute(near_rows[k - 1], AXES, same)
         if k < far:
@@ -219,11 +239,11 @@
         if k < far - 1:
             far_sum = lax.ppermute(far_sum, AXES, same_back)
             far_sum = add(far_sum, partial["far", k])
+    lengths, near_sum = lax.optimization_barrier((lengths, near_sum))
     near_sum = lax.ppermute(near_sum, AXES, same_back)
     far_sum = lax.ppermute(far_sum, AXES, cross_back)
-    lengths, own_part = lax.optimization_barrier((lengths, partial["own", 0]))
     attn_out = attend(queries, k_cache, value_cache, lengths)
-    routed_out = add(near_sum, far_sum, own_part)
+    routed_out = add(near_sum, far_sum, partial["own", 0])
     return (routed_out, attn_out)
 
 

time: 77.4 us -> 73.8 us (0.953)
  Pallas kernels: 23.8 us -> 18.3 us
  starting transfers between devices: 18 us -> 23.2 us
  waiting for transfers between devices: 30.9 us -> 27.1 us
    ppermute x4, starting transfers between devices: 1.5 us -> 7.24 us  [local(): near_sum = lax.ppermute(near_sum, AXES, same_back)]
    ppermute x4, waiting for transfers between devices: 13.8 us -> 8.16 us  [local(): near_sum = lax.ppermute(near_sum, AXES, same_back)]
    pallas_call x2 -> x1, Pallas kernels: 8.66 us -> 4.33 us  [stage(): pl.pallas_call(stage_kernel, out_shape=[pltpu.VMEM((slots, width, 2 * hal...]
    ppermute x3, waiting for transfers between devices: 5.13 us -> 9.46 us  [local(): near_rows[k] = lax.ppermute(near_rows[k - 1], AXES, same)]
    ppermute x2, waiting for transfers between devices: 4.75 us -> 1 us  [local(): far_sum = lax.ppermute(far_sum, AXES, same_back)]
    ppermute x2, waiting for transfers between devices: 1.28 us -> 3.33 us  [local(): far_rows[k] = lax.ppermute(far_rows[k - 1], AXES, same)]
    dot_general x1, matrix products: 0.36 us -> 1.69 us  [attend(): jnp.einsum('rkgl,rlkd->rkgd', probs, value_cache, preferred_element_type=...]
    ppermute x2, starting transfers between devices: 2.41 us -> 3.26 us  [local(): far_sum = lax.ppermute(far_sum, AXES, same_back)]
  transfers between devices with their start and end apart: 17 -> 16, of which waited for: 11 -> 10; matrix products, arithmetic and copies ran while one was open for 4% -> 5% of each run, Pallas kernels for 24% -> 13%
where the time goes in v1:
time: 73.8 us; the launch traced here: 73.6 us
  waiting for transfers between devices  27.1 us (37%)
  starting transfers between devices  23.2 us (31%)
  Pallas kernels  18.3 us (25%)
  matrix products  2.38 us (3%)
  other arithmetic  1.27 us (2%)
  between operations  0.77 us (1%)
    pallas_call x3, Pallas kernels, expert(): pl.pallas_call(functools.partial(expert_kernel, count, sources, base, boo...  12.9 us
    ppermute x3, waiting for transfers between devices, local(): near_rows[k] = lax.ppermute(near_rows[k - 1], AXES, same)  9.46 us
    ppermute x4, waiting for transfers between devices, local(): near_sum = lax.ppermute(near_sum, AXES, same_back)  8.16 us
    ppermute x4, starting transfers between devices, local(): near_sum = lax.ppermute(near_sum, AXES, same_back)  7.24 us
    ppermute x1, waiting for transfers between devices, local(): near_rows[1] = lax.ppermute(own, AXES, same)  5.12 us
    ppermute x3, starting transfers between devices, local(): near_rows[k] = lax.ppermute(near_rows[k - 1], AXES, same)  5.11 us
    pallas_call x1, Pallas kernels, stage(): pl.pallas_call(stage_kernel, out_shape=[pltpu.VMEM((slots, width, 2 * hal...  4.33 us
    ppermute x2, waiting for transfers between devices, local(): far_rows[k] = lax.ppermute(far_rows[k - 1], AXES, same)  3.33 us
  transfers between devices with their start and end apart: 16, of which 10 were waited for; matrix products, arithmetic and copies ran while one was open for 5% of the time, Pallas kernels for 13%

profile of v1, /device:TPU:0, one launch (start us, length us, event | category | flops | bytes accessed | tf_op | source)
XLA Modules:
  0.0 73.6 jit_solution(14646496689300697692)
XLA Ops:
  0.6 0.0 copy-start
  0.7 0.1 pad_add_fusion.first_ref
  0.7 4.3 %stage.1 = (bf16[2,2048,768]{2,1,0:T(8,128)(2,1)S(1)}, bf16[2,384,2048]{2,1,0:T(8,128)(2,1)S(1)}) custom-call(s32[2]{0:T(128)S(1)} %pad_add_fusion.first_ref, bf16[2,2048,384]{2,1,0:T(8,128)(2,1)} %gate.1, bf16[2,2048,384]{2,1,0:T(8,128)(2,1)} %up.1, bf16[2,384,2048]{2,1,0:T(8,128)(2,1)} %down.1), custom_call_target="tpu_custom_call" | custom-call | tf_op jit(solution)/shard_map/stage/pallas_call | solution.py:96
  5.1 0.6 collective-permute-start.7
  5.6 0.1 collective-permute-start.8
  5.7 1.0 %pack.1.refs_0_ = bf16[64,2176]{1,0:T(8,128)(2,1)S(1)} custom-call(bf16[64,2048]{1,0:T(8,128)(2,1)} %tokens.1, bf16[8,64]{1,0:T(8,128)(2,1)} %bitcast.19, s32[8,64]{1,0:T(8,128)} %bitcast.17, s32[8,64]{1,0:T(8,128)} %bitcast.18), custom_call_target="tpu_custom_call" | custom-call | tf_op jit(solution)/shard_map/pack/pallas_call | solution.py:64
  6.7 3.0 %collective-permute-start = (bf16[64,2176]{1,0:T(8,128)(2,1)S(1)}, bf16[64,2176]{1,0:T(8,128)(2,1)S(1)}, u32[]{:S(2)}, u32[]{:S(2)}) collective-permute-start(bf16[64,2176]{1,0:T(8,128)(2,1)S(1)} %pack.1.refs_0_), channel_id=1, source_target_pairs={{0,4},{4,8},{8,12},{12,14},{14,10},{10,6},{6,2},{2,0},{5,1},{9,5},... | collective-permute-start | bytes 835592 | tf_op jit(solution)/shard_map/ppermute | solution.py:204
  9.8 0.9 %collective-permute-start.3 = (bf16[64,2176]{1,0:T(8,128)(2,1)S(1)}, bf16[64,2176]{1,0:T(8,128)(2,1)S(1)}, u32[]{:S(2)}, u32[]{:S(2)}) collective-permute-start(bf16[64,2176]{1,0:T(8,128)(2,1)S(1)} %pack.1.refs_0_), channel_id=1, source_target_pairs={{1,4},{5,8},{9,12},{13,14},{15,10},{11,6},{7,2},{3,0},{4,1},{8,5},... | collective-permute-start | bytes 835592 | tf_op jit(solution)/shard_map/ppermute | solution.py:205
  10.7 5.1 %collective-permute-done.refs_1_ = bf16[64,2176]{1,0:T(8,128)(2,1)S(1)} collective-permute-done((bf16[64,2176]{1,0:T(8,128)(2,1)S(1)}, bf16[64,2176]{1,0:T(8,128)(2,1)S(1)}, u32[]{:S(2)}, u32[]{:S(2)}) %collective-permute-start) | collective-permute-done | bytes 278560 | tf_op jit(solution)/shard_map/ppermute | solution.py:204
  15.8 2.5 %collective-permute-start.1 = (bf16[64,2176]{1,0:T(8,128)(2,1)S(1)}, bf16[64,2176]{1,0:T(8,128)(2,1)S(1)}, u32[]{:S(2)}, u32[]{:S(2)}) collective-permute-start(bf16[64,2176]{1,0:T(8,128)(2,1)S(1)} %collective-permute-done.refs_1_), channel_id=1, source_target_pairs={{0,4},{4,8},{8,12},{12,14},{14,10},{10,6},{6,2},{2,0},{5,1},{9,5},... | collective-permute-start | bytes 835592 | tf_op jit(solution)/shard_map/ppermute | solution.py:211
  18.3 0.0 collective-permute-done.3.refs_2_
  18.3 1.6 %collective-permute-start.4 = (bf16[64,2176]{1,0:T(8,128)(2,1)S(1)}, bf16[64,2176]{1,0:T(8,128)(2,1)S(1)}, u32[]{:S(2)}, u32[]{:S(2)}) collective-permute-start(bf16[64,2176]{1,0:T(8,128)(2,1)S(1)} %collective-permute-done.3.refs_2_), channel_id=1, source_target_pairs={{0,4},{4,8},{8,12},{12,14},{14,10},{10,6},{6,2},{2,0},{5,1},{9,5},... | collective-permute-start | bytes 835592 | tf_op jit(solution)/shard_map/ppermute | solution.py:213
  19.9 3.6 %collective-permute-done.1.refs_3_ = bf16[64,2176]{1,0:T(8,128)(2,1)S(1)} collective-permute-done((bf16[64,2176]{1,0:T(8,128)(2,1)S(1)}, bf16[64,2176]{1,0:T(8,128)(2,1)S(1)}, u32[]{:S(2)}, u32[]{:S(2)}) %collective-permute-start.1) | collective-permute-done | bytes 278560 | tf_op jit(solution)/shard_map/ppermute | solution.py:211
  23.5 1.3 %collective-permute-start.2 = (bf16[64,2176]{1,0:T(8,128)(2,1)S(1)}, bf16[64,2176]{1,0:T(8,128)(2,1)S(1)}, u32[]{:S(2)}, u32[]{:S(2)}) collective-permute-start(bf16[64,2176]{1,0:T(8,128)(2,1)S(1)} %collective-permute-done.1.refs_3_), channel_id=1, source_target_pairs={{0,4},{4,8},{8,12},{12,14},{14,10},{10,6},{6,2},{2,0},{5,1},{9,5},... | collective-permute-start | bytes 835592 | tf_op jit(solution)/shard_map/ppermute | solution.py:211
  24.9 1.7 %collective-permute-done.4.refs_4_ = bf16[64,2176]{1,0:T(8,128)(2,1)S(1)} collective-permute-done((bf16[64,2176]{1,0:T(8,128)(2,1)S(1)}, bf16[64,2176]{1,0:T(8,128)(2,1)S(1)}, u32[]{:S(2)}, u32[]{:S(2)}) %collective-permute-start.4) | collective-permute-done | bytes 278560 | tf_op jit(solution)/shard_map/ppermute | solution.py:213
  26.5 1.3 %collective-permute-start.5 = (bf16[64,2176]{1,0:T(8,128)(2,1)S(1)}, bf16[64,2176]{1,0:T(8,128)(2,1)S(1)}, u32[]{:S(2)}, u32[]{:S(2)}) collective-permute-start(bf16[64,2176]{1,0:T(8,128)(2,1)S(1)} %collective-permute-done.4.refs_4_), channel_id=1, source_target_pairs={{0,4},{4,8},{8,12},{12,14},{14,10},{10,6},{6,2},{2,0},{5,1},{9,5},... | collective-permute-start | bytes 835592 | tf_op jit(solution)/shard_map/ppermute | solution.py:213
  27.8 2.2 %collective-permute-done.2.refs_0_ = bf16[64,2176]{1,0:T(8,128)(2,1)S(1)} collective-permute-done((bf16[64,2176]{1,0:T(8,128)(2,1)S(1)}, bf16[64,2176]{1,0:T(8,128)(2,1)S(1)}, u32[]{:S(2)}, u32[]{:S(2)}) %collective-permute-start.2) | collective-permute-done | bytes 278560 | tf_op jit(solution)/shard_map/ppermute | solution.py:211
  30.1 1.3 %collective-permute-start.6 = (bf16[64,2176]{1,0:T(8,128)(2,1)S(1)}, bf16[64,2176]{1,0:T(8,128)(2,1)S(1)}, u32[]{:S(2)}, u32[]{:S(2)}) collective-permute-start(bf16[64,2176]{1,0:T(8,128)(2,1)S(1)} %collective-permute-done.2.refs_0_), channel_id=1, source_target_pairs={{0,4},{4,8},{8,12},{12,14},{14,10},{10,6},{6,2},{2,0},{5,1},{9,5},... | collective-permute-start | bytes 835592 | tf_op jit(solution)/shard_map/ppermute | solution.py:211
  31.4 1.7 %collective-permute-done.5.refs_1_ = bf16[64,2176]{1,0:T(8,128)(2,1)S(1)} collective-permute-done((bf16[64,2176]{1,0:T(8,128)(2,1)S(1)}, bf16[64,2176]{1,0:T(8,128)(2,1)S(1)}, u32[]{:S(2)}, u32[]{:S(2)}) %collective-permute-start.5) | collective-permute-done | bytes 278560 | tf_op jit(solution)/shard_map/ppermute | solution.py:213
  33.1 3.6 %collective-permute-done.6.refs_2_ = bf16[64,2176]{1,0:T(8,128)(2,1)S(1)} collective-permute-done((bf16[64,2176]{1,0:T(8,128)(2,1)S(1)}, bf16[64,2176]{1,0:T(8,128)(2,1)S(1)}, u32[]{:S(2)}, u32[]{:S(2)}) %collective-permute-start.6) | collective-permute-done | bytes 278560 | tf_op jit(solution)/shard_map/ppermute | solution.py:211
  36.6 0.0 collective-permute-done.8.refs_6_
  36.6 0.0 collective-permute-done.7.refs_5_
  36.6 4.7 %expert.3 = (bf16[64,2048]{1,0:T(8,128)(2,1)S(1)}, bf16[64,2048]{1,0:T(8,128)(2,1)S(1)}, bf16[64,2048]{1,0:T(8,128)(2,1)S(1)}) custom-call(s32[2]{0:T(128)S(1)} %pad_add_fusion.first_ref, bf16[64,2176]{1,0:T(8,128)(2,1)S(1)} %collective-permute-done.2.refs_0_, bf16[64,2176]{1,0:T(8,128)(2,1)S(1)} %collective-permute-done.5.refs_1_, ...), custom_call_target="tpu_custom_call" | custom-call | tf_op jit(solution)/shard_map/expert/pallas_call | solution.py:155
  41.4 2.1 %collective-permute-start.9 = (bf16[64,2048]{1,0:T(8,128)(2,1)S(1)}, bf16[64,2048]{1,0:T(8,128)(2,1)S(1)}, u32[]{:S(2)}, u32[]{:S(2)}) collective-permute-start(bf16[64,2048]{1,0:T(8,128)(2,1)S(1)} %get-tuple-element.21), channel_id=1, source_target_pairs={{4,0},{8,4},{12,8},{14,12},{10,14},{6,10},{2,6},{0,2},{1,5},{5,9},... | collective-permute-start | bytes 786440 | tf_op jit(solution)/shard_map/ppermute | solution.py:237
  43.4 4.1 %expert.4 = (f32[64,2048]{1,0:T(8,128)S(1)}, f32[64,2048]{1,0:T(8,128)S(1)}, f32[64,2048]{1,0:T(8,128)S(1)}, f32[64,2048]{1,0:T(8,128)S(1)}, f32[64,2048]{1,0:T(8,128)S(1)}) custom-call(s32[2]{0:T(128)S(1)} %pad_add_fusion.first_ref, bf16[64,2176]{1,0:T(8,128)(2,1)S(1)} %pack.1.refs_0_, bf16[64,2176]{1,0:T(8,128)(2,1)S(1)} %collective-permute-done.refs_1_, ...), custom_call_target="tpu_custom_call" | custom-call | tf_op jit(solution)/shard_map/expert/pallas_call | solution.py:155
  47.5 1.6 %collective-permute-start.13 = (bf16[64,2048]{1,0:T(8,128)(2,1)S(1)}, bf16[64,2048]{1,0:T(8,128)(2,1)S(1)}, u32[]{:S(2)}, u32[]{:S(2)}) collective-permute-start(bf16[64,2048]{1,0:T(8,128)(2,1)S(1)} %get-tuple-element.31), channel_id=1, source_target_pairs={{4,0},{8,4},{12,8},{14,12},{10,14},{6,10},{2,6},{0,2},{1,5},{5,9},... | collective-permute-start | bytes 786440 | tf_op jit(solution)/shard_map/ppermute | solution.py:240
  49.2 4.1 %expert.5 = (bf16[64,2048]{1,0:T(8,128)(2,1)S(1)}, bf16[64,2048]{1,0:T(8,128)(2,1)S(1)}, bf16[64,2048]{1,0:T(8,128)(2,1)S(1)}, bf16[64,2048]{1,0:T(8,128)(2,1)S(1)}, bf16[64,2048]{1,0:T(8,128)(2,1)S(1)}) custom-call(s32[2]{0:T(128)S(1)} %pad_add_fusion.first_ref, bf16[64,2176]{1,0:T(8,128)(2,1)S(1)} %pack.1.refs_0_, ...), custom_call_target="tpu_custom_call" | custom-call | tf_op jit(solution)/shard_map/expert/pallas_call | solution.py:155
  53.3 0.0 collective-permute-done.9
  53.3 0.1 add_convert_fusion.5
  53.4 1.7 %collective-permute-start.10 = (bf16[64,2048]{1,0:T(8,128)(2,1)S(1)}, bf16[64,2048]{1,0:T(8,128)(2,1)S(1)}, u32[]{:S(2)}, u32[]{:S(2)}) collective-permute-start(bf16[64,2048]{1,0:T(8,128)(2,1)S(1)} %add_convert_fusion.5), channel_id=1, source_target_pairs={{4,0},{8,4},{12,8},{14,12},{10,14},{6,10},{2,6},{0,2},{1,5},{5,9},... | collective-permute-start | bytes 786440 | tf_op jit(solution)/shard_map/ppermute | solution.py:237
  55.1 0.0 collective-permute-done.13
  55.1 0.1 add_convert_fusion.2
  55.2 0.0 copy-start.1
  55.2 0.0 copy-start.2
  55.2 1.6 %collective-permute-start.14 = (bf16[64,2048]{1,0:T(8,128)(2,1)S(1)}, bf16[64,2048]{1,0:T(8,128)(2,1)S(1)}, u32[]{:S(2)}, u32[]{:S(2)}) collective-permute-start(bf16[64,2048]{1,0:T(8,128)(2,1)S(1)} %add_convert_fusion.2), channel_id=1, source_target_pairs={{4,0},{8,4},{12,8},{14,12},{10,14},{6,10},{2,6},{0,2},{1,5},{5,9},... | collective-permute-start | bytes 786440 | tf_op jit(solution)/shard_map/ppermute | solution.py:240
  56.8 3.0 %collective-permute-done.10 = bf16[64,2048]{1,0:T(8,128)(2,1)S(1)} collective-permute-done((bf16[64,2048]{1,0:T(8,128)(2,1)S(1)}, bf16[64,2048]{1,0:T(8,128)(2,1)S(1)}, u32[]{:S(2)}, u32[]{:S(2)}) %collective-permute-start.10) | collective-permute-done | bytes 262176 | tf_op jit(solution)/shard_map/ppermute | solution.py:237
  59.8 0.1 add_convert_fusion.4
  59.9 1.7 %collective-permute-start.11 = (bf16[64,2048]{1,0:T(8,128)(2,1)S(1)}, bf16[64,2048]{1,0:T(8,128)(2,1)S(1)}, u32[]{:S(2)}, u32[]{:S(2)}) collective-permute-start(bf16[64,2048]{1,0:T(8,128)(2,1)S(1)} %add_convert_fusion.4), channel_id=1, source_target_pairs={{4,0},{8,4},{12,8},{14,12},{10,14},{6,10},{2,6},{0,2},{1,5},{5,9},... | collective-permute-start | bytes 786440 | tf_op jit(solution)/shard_map/ppermute | solution.py:237
  61.6 1.0 %collective-permute-done.14 = bf16[64,2048]{1,0:T(8,128)(2,1)S(1)} collective-permute-done((bf16[64,2048]{1,0:T(8,128)(2,1)S(1)}, bf16[64,2048]{1,0:T(8,128)(2,1)S(1)}, u32[]{:S(2)}, u32[]{:S(2)}) %collective-permute-start.14) | collective-permute-done | bytes 262176 | tf_op jit(solution)/shard_map/ppermute | solution.py:240
  62.6 0.1 add_convert_fusion.1
  62.7 0.1 collective-permute-start.15
  62.7 3.5 %collective-permute-done.11 = bf16[64,2048]{1,0:T(8,128)(2,1)S(1)} collective-permute-done((bf16[64,2048]{1,0:T(8,128)(2,1)S(1)}, bf16[64,2048]{1,0:T(8,128)(2,1)S(1)}, u32[]{:S(2)}, u32[]{:S(2)}) %collective-permute-start.11) | collective-permute-done | bytes 262176 | tf_op jit(solution)/shard_map/ppermute | solution.py:237
  66.3 0.1 add_convert_fusion.3
  66.4 0.0 copy-done.1
  66.4 0.1 iota_compare_fusion
  66.4 1.7 %collective-permute-start.12 = (bf16[64,2048]{1,0:T(8,128)(2,1)S(1)}, bf16[64,2048]{1,0:T(8,128)(2,1)S(1)}, u32[]{:S(2)}, u32[]{:S(2)}) collective-permute-start(bf16[64,2048]{1,0:T(8,128)(2,1)S(1)} %add_convert_fusion.3), channel_id=1, source_target_pairs={{4,0},{8,4},{12,8},{14,12},{10,14},{6,10},{2,6},{0,2},{1,5},{5,9},... | collective-permute-start | bytes 786440 | tf_op jit(solution)/shard_map/ppermute | solution.py:243
  68.1 0.0 copy-done
  68.1 0.0 copy-done.2
  68.1 0.7 fusion.22
  68.8 1.7 %fusion.17 = bf16[1,2,32,128]{3,2,1,0:T(8,128)(2,1)S(1)} fusion(bf16[2,640,4,128]{3,2,1,0:T(4,128)(2,1)} %param.20, f32[2,4,8,640]{3,2,1,0:T(8,128)S(1)} %get-tuple-element.37, f32[2,4,8]{2,1,0:T(4,128)S(1)} %get-tuple-element.36), kind=kOutput, calls=%fused_computation.11 | convolution fusion | flops 10575872 | bytes 1491200 | tf_op jit(solution)/shard_map/rkgl,rlkd->rkgd/dot_general | solution.py:31
  70.5 0.6 copy.31
  71.1 0.0 collective-permute-done.15
  71.1 1.7 %collective-permute-done.12 = bf16[64,2048]{1,0:T(8,128)(2,1)S(1)} collective-permute-done((bf16[64,2048]{1,0:T(8,128)(2,1)S(1)}, bf16[64,2048]{1,0:T(8,128)(2,1)S(1)}, u32[]{:S(2)}, u32[]{:S(2)}) %collective-permute-start.12) | collective-permute-done | bytes 262176 | tf_op jit(solution)/shard_map/ppermute | solution.py:243
  72.8 0.8 %add_convert_fusion = bf16[64,2048]{1,0:T(8,128)(2,1)} fusion(bf16[64,2048]{1,0:T(8,128)(2,1)S(1)} %get-tuple-element.34, bf16[64,2048]{1,0:T(8,128)(2,1)S(1)} %collective-permute-done.15, bf16[64,2048]{1,0:T(8,128)(2,1)S(1)} %collective-permute-done.12), kind=kLoop, calls=%fused_computation.12 | loop fusion | flops 786432 | bytes 1048576 | tf_op jit(solution)/shard_map/convert_element_type | solution.py:251
Async XLA Ops:
  0.6 67.5 %copy-start = (bf16[2,640,4,128]{3,2,1,0:T(4,128)(2,1)S(1)}, bf16[2,640,4,128]{3,2,1,0:T(4,128)(2,1)}, u32[]{:S(2)}) copy-start(bf16[2,640,4,128]{3,2,1,0:T(4,128)(2,1)} %param.19) | copy-start | bytes 3932164
  5.1 31.6 %collective-permute-start.7 = (bf16[2,2048,768]{2,1,0:T(8,128)(2,1)S(1)}, bf16[2,2048,768]{2,1,0:T(8,128)(2,1)S(1)}, u32[]{:S(2)}, u32[]{:S(2)}) collective-permute-start(bf16[2,2048,768]{2,1,0:T(8,128)(2,1)S(1)} %get-tuple-element.19.refs_3_.refs_5_), channel_id=1, source_target_pairs={{0,1},{1,0},{2,3},{3,2},{4,5},{5,4},{6,7},{7,6},{8,9},{9,8},{10,11... | collective-permute-start | bytes 18874376 | tf_op jit(solution)/shard_map/ppermute | solution.py:209
  5.6 31.0 %collective-permute-start.8 = (bf16[2,384,2048]{2,1,0:T(8,128)(2,1)S(1)}, bf16[2,384,2048]{2,1,0:T(8,128)(2,1)S(1)}, u32[]{:S(2)}, u32[]{:S(2)}) collective-permute-start(bf16[2,384,2048]{2,1,0:T(8,128)(2,1)S(1)} %get-tuple-element.20.refs_4_.refs_6_), channel_id=1, source_target_pairs={{0,1},{1,0},{2,3},{3,2},{4,5},{5,4},{6,7},{7,6},{8,9},{9,8},{10,11... | collective-permute-start | bytes 9437192 | tf_op jit(solution)/shard_map/ppermute | solution.py:209
  6.7 9.1 %collective-permute-start = (bf16[64,2176]{1,0:T(8,128)(2,1)S(1)}, bf16[64,2176]{1,0:T(8,128)(2,1)S(1)}, u32[]{:S(2)}, u32[]{:S(2)}) collective-permute-start(bf16[64,2176]{1,0:T(8,128)(2,1)S(1)} %pack.1.refs_0_), channel_id=1, source_target_pairs={{0,4},{4,8},{8,12},{12,14},{14,10},{10,6},{6,2},{2,0},{5,1},{9,5},... | collective-permute-start | bytes 835592 | tf_op jit(solution)/shard_map/ppermute | solution.py:204
  9.8 8.5 %collective-permute-start.3 = (bf16[64,2176]{1,0:T(8,128)(2,1)S(1)}, bf16[64,2176]{1,0:T(8,128)(2,1)S(1)}, u32[]{:S(2)}, u32[]{:S(2)}) collective-permute-start(bf16[64,2176]{1,0:T(8,128)(2,1)S(1)} %pack.1.refs_0_), channel_id=1, source_target_pairs={{1,4},{5,8},{9,12},{13,14},{15,10},{11,6},{7,2},{3,0},{4,1},{8,5},... | collective-permute-start | bytes 835592 | tf_op jit(solution)/shard_map/ppermute | solution.py:205
  15.8 7.7 %collective-permute-start.1 = (bf16[64,2176]{1,0:T(8,128)(2,1)S(1)}, bf16[64,2176]{1,0:T(8,128)(2,1)S(1)}, u32[]{:S(2)}, u32[]{:S(2)}) collective-permute-start(bf16[64,2176]{1,0:T(8,128)(2,1)S(1)} %collective-permute-done.refs_1_), channel_id=1, source_target_pairs={{0,4},{4,8},{8,12},{12,14},{14,10},{10,6},{6,2},{2,0},{5,1},{9,5},... | collective-permute-start | bytes 835592 | tf_op jit(solution)/shard_map/ppermute | solution.py:211
  18.3 8.2 %collective-permute-start.4 = (bf16[64,2176]{1,0:T(8,128)(2,1)S(1)}, bf16[64,2176]{1,0:T(8,128)(2,1)S(1)}, u32[]{:S(2)}, u32[]{:S(2)}) collective-permute-start(bf16[64,2176]{1,0:T(8,128)(2,1)S(1)} %collective-permute-done.3.refs_2_), channel_id=1, source_target_pairs={{0,4},{4,8},{8,12},{12,14},{14,10},{10,6},{6,2},{2,0},{5,1},{9,5},... | collective-permute-start | bytes 835592 | tf_op jit(solution)/shard_map/ppermute | solution.py:213
  23.5 6.5 %collective-permute-start.2 = (bf16[64,2176]{1,0:T(8,128)(2,1)S(1)}, bf16[64,2176]{1,0:T(8,128)(2,1)S(1)}, u32[]{:S(2)}, u32[]{:S(2)}) collective-permute-start(bf16[64,2176]{1,0:T(8,128)(2,1)S(1)} %collective-permute-done.1.refs_3_), channel_id=1, source_target_pairs={{0,4},{4,8},{8,12},{12,14},{14,10},{10,6},{6,2},{2,0},{5,1},{9,5},... | collective-permute-start | bytes 835592 | tf_op jit(solution)/shard_map/ppermute | solution.py:211
  26.5 6.5 %collective-permute-start.5 = (bf16[64,2176]{1,0:T(8,128)(2,1)S(1)}, bf16[64,2176]{1,0:T(8,128)(2,1)S(1)}, u32[]{:S(2)}, u32[]{:S(2)}) collective-permute-start(bf16[64,2176]{1,0:T(8,128)(2,1)S(1)} %collective-permute-done.4.refs_4_), channel_id=1, source_target_pairs={{0,4},{4,8},{8,12},{12,14},{14,10},{10,6},{6,2},{2,0},{5,1},{9,5},... | collective-permute-start | bytes 835592 | tf_op jit(solution)/shard_map/ppermute | solution.py:213
  30.1 6.5 %collective-permute-start.6 = (bf16[64,2176]{1,0:T(8,128)(2,1)S(1)}, bf16[64,2176]{1,0:T(8,128)(2,1)S(1)}, u32[]{:S(2)}, u32[]{:S(2)}) collective-permute-start(bf16[64,2176]{1,0:T(8,128)(2,1)S(1)} %collective-permute-done.2.refs_0_), channel_id=1, source_target_pairs={{0,4},{4,8},{8,12},{12,14},{14,10},{10,6},{6,2},{2,0},{5,1},{9,5},... | collective-permute-start | bytes 835592 | tf_op jit(solution)/shard_map/ppermute | solution.py:211
  41.4 11.9 %collective-permute-start.9 = (bf16[64,2048]{1,0:T(8,128)(2,1)S(1)}, bf16[64,2048]{1,0:T(8,128)(2,1)S(1)}, u32[]{:S(2)}, u32[]{:S(2)}) collective-permute-start(bf16[64,2048]{1,0:T(8,128)(2,1)S(1)} %get-tuple-element.21), channel_id=1, source_target_pairs={{4,0},{8,4},{12,8},{14,12},{10,14},{6,10},{2,6},{0,2},{1,5},{5,9},... | collective-permute-start | bytes 786440 | tf_op jit(solution)/shard_map/ppermute | solution.py:237
  47.5 7.6 %collective-permute-start.13 = (bf16[64,2048]{1,0:T(8,128)(2,1)S(1)}, bf16[64,2048]{1,0:T(8,128)(2,1)S(1)}, u32[]{:S(2)}, u32[]{:S(2)}) collective-permute-start(bf16[64,2048]{1,0:T(8,128)(2,1)S(1)} %get-tuple-element.31), channel_id=1, source_target_pairs={{4,0},{8,4},{12,8},{14,12},{10,14},{6,10},{2,6},{0,2},{1,5},{5,9},... | collective-permute-start | bytes 786440 | tf_op jit(solution)/shard_map/ppermute | solution.py:240
  53.4 6.4 %collective-permute-start.10 = (bf16[64,2048]{1,0:T(8,128)(2,1)S(1)}, bf16[64,2048]{1,0:T(8,128)(2,1)S(1)}, u32[]{:S(2)}, u32[]{:S(2)}) collective-permute-start(bf16[64,2048]{1,0:T(8,128)(2,1)S(1)} %add_convert_fusion.5), channel_id=1, source_target_pairs={{4,0},{8,4},{12,8},{14,12},{10,14},{6,10},{2,6},{0,2},{1,5},{5,9},... | collective-permute-start | bytes 786440 | tf_op jit(solution)/shard_map/ppermute | solution.py:237
  55.2 11.2 %copy-start.1 = (s32[2]{0:T(128)S(1)}, s32[2]{0:T(128)}, u32[]{:S(2)}) copy-start(s32[2]{0:T(128)} %param.21) | copy-start | bytes 28
  55.2 12.9 %copy-start.2 = (bf16[2,32,128]{2,1,0:T(8,128)(2,1)S(1)}, bf16[2,32,128]{2,1,0:T(8,128)(2,1)}, u32[]{:S(2)}) copy-start(bf16[2,32,128]{2,1,0:T(8,128)(2,1)} %param.18) | copy-start | bytes 49156
  55.2 7.4 %collective-permute-start.14 = (bf16[64,2048]{1,0:T(8,128)(2,1)S(1)}, bf16[64,2048]{1,0:T(8,128)(2,1)S(1)}, u32[]{:S(2)}, u32[]{:S(2)}) collective-permute-start(bf16[64,2048]{1,0:T(8,128)(2,1)S(1)} %add_convert_fusion.2), channel_id=1, source_target_pairs={{4,0},{8,4},{12,8},{14,12},{10,14},{6,10},{2,6},{0,2},{1,5},{5,9},... | collective-permute-start | bytes 786440 | tf_op jit(solution)/shard_map/ppermute | solution.py:240
  59.9 6.4 %collective-permute-start.11 = (bf16[64,2048]{1,0:T(8,128)(2,1)S(1)}, bf16[64,2048]{1,0:T(8,128)(2,1)S(1)}, u32[]{:S(2)}, u32[]{:S(2)}) collective-permute-start(bf16[64,2048]{1,0:T(8,128)(2,1)S(1)} %add_convert_fusion.4), channel_id=1, source_target_pairs={{4,0},{8,4},{12,8},{14,12},{10,14},{6,10},{2,6},{0,2},{1,5},{5,9},... | collective-permute-start | bytes 786440 | tf_op jit(solution)/shard_map/ppermute | solution.py:237
  62.7 8.5 %collective-permute-start.15 = (bf16[64,2048]{1,0:T(8,128)(2,1)S(1)}, bf16[64,2048]{1,0:T(8,128)(2,1)S(1)}, u32[]{:S(2)}, u32[]{:S(2)}) collective-permute-start(bf16[64,2048]{1,0:T(8,128)(2,1)S(1)} %add_convert_fusion.1), channel_id=1, source_target_pairs={{4,1},{8,5},{12,9},{14,13},{10,15},{6,11},{2,7},{0,3},{1,4},{5,8},... | collective-permute-start | bytes 786440 | tf_op jit(solution)/shard_map/ppermute | solution.py:244
  66.4 6.4 %collective-permute-start.12 = (bf16[64,2048]{1,0:T(8,128)(2,1)S(1)}, bf16[64,2048]{1,0:T(8,128)(2,1)S(1)}, u32[]{:S(2)}, u32[]{:S(2)}) collective-permute-start(bf16[64,2048]{1,0:T(8,128)(2,1)S(1)} %add_convert_fusion.3), channel_id=1, source_target_pairs={{4,0},{8,4},{12,8},{14,12},{10,14},{6,10},{2,6},{0,2},{1,5},{5,9},... | collective-permute-start | bytes 786440 | tf_op jit(solution)/shard_map/ppermute | solution.py:243

commit v2 on v1

--- a/solution.py
+++ b/solution.py
@@ -171,9 +171,13 @@
 
 def permutations(chips):
     ring = list(range(0, chips, 2)) + list(range(chips - 1 - chips % 2, 0, -2))
-    step = {ring[i]: ring[(i + 1) % chips] for i in range(chips)}
-    same = [(2 * a, 2 * b) for a, b in step.items()] + [(2 * b + 1, 2 * a + 1) for a, b in step.items()]
-    cross = [(2 * a + 1, 2 * b) for a, b in step.items()] + [(2 * b, 2 * a + 1) for a, b in step.items()]
+    ups = [2 * chip + place % 2 for place, chip in enumerate(ring)]
+    downs = [2 * chip + (place + 1) % 2 for place, chip in enumerate(ring)]
+    same, cross = [], []
+    for place in range(chips):
+        after = (place + 1) % chips
+        same += [(ups[place], ups[after]), (downs[after], downs[place])]
+        cross += [(downs[place], ups[after]), (ups[after], downs[place])]
     return same, cross, [(b, a) for a, b in same], [(b, a) for a, b in cross]
 
 

time: 73.8 us -> 70 us (0.949)
  waiting for transfers between devices: 27.1 us -> 23 us
    ppermute x3, waiting for transfers between devices: 9.46 us -> 8.19 us  [local(): near_rows[k] = lax.ppermute(near_rows[k - 1], AXES, same)]
    ppermute x2, waiting for transfers between devices: 3.33 us -> 2.11 us  [local(): far_rows[k] = lax.ppermute(far_rows[k - 1], AXES, same)]
    ppermute x2, starting transfers between devices: 3.26 us -> 2.12 us  [local(): far_sum = lax.ppermute(far_sum, AXES, same_back)]
    ppermute x3, starting transfers between devices: 5.11 us -> 6.06 us  [local(): near_rows[k] = lax.ppermute(near_rows[k - 1], AXES, same)]
where the time goes in v2:
time: 70 us; the launch traced here: 69.8 us
  starting transfers between devices  23.4 us (33%)
  waiting for transfers between devices  23 us (33%)
  Pallas kernels  18.3 us (26%)
  matrix products  2.38 us (3%)
  other arithmetic  1.27 us (2%)
  between operations  0.77 us (1%)
    pallas_call x3, Pallas kernels, expert(): pl.pallas_call(functools.partial(expert_kernel, count, sources, base, boo...  12.9 us
    ppermute x3, waiting for transfers between devices, local(): near_rows[k] = lax.ppermute(near_rows[k - 1], AXES, same)  8.19 us
    ppermute x4, waiting for transfers between devices, local(): near_sum = lax.ppermute(near_sum, AXES, same_back)  7.6 us
    ppermute x4, starting transfers between devices, local(): near_sum = lax.ppermute(near_sum, AXES, same_back)  7.59 us
    ppermute x3, starting transfers between devices, local(): near_rows[k] = lax.ppermute(near_rows[k - 1], AXES, same)  6.06 us
    ppermute x1, waiting for transfers between devices, local(): near_rows[1] = lax.ppermute(own, AXES, same)  4.49 us
    pallas_call x1, Pallas kernels, stage(): pl.pallas_call(stage_kernel, out_shape=[pltpu.VMEM((slots, width, 2 * hal...  4.33 us
    ppermute x1, starting transfers between devices, local(): near_rows[1] = lax.ppermute(own, AXES, same)  2.73 us
  transfers between devices with their start and end apart: 16, of which 10 were waited for; matrix products, arithmetic and copies ran while one was open for 5% of the time, Pallas kernels for 13%

profile of v2, /device:TPU:0, one launch (start us, length us, event | category | flops | bytes accessed | tf_op | source)
XLA Modules:
  0.0 69.8 jit_solution(13484755514465054559)
XLA Ops:
  0.6 0.0 copy-start
  0.7 0.1 pad_add_fusion.first_ref
  0.7 4.3 %stage.1 = (bf16[2,2048,768]{2,1,0:T(8,128)(2,1)S(1)}, bf16[2,384,2048]{2,1,0:T(8,128)(2,1)S(1)}) custom-call(s32[2]{0:T(128)S(1)} %pad_add_fusion.first_ref, bf16[2,2048,384]{2,1,0:T(8,128)(2,1)} %gate.1, bf16[2,2048,384]{2,1,0:T(8,128)(2,1)} %up.1, bf16[2,384,2048]{2,1,0:T(8,128)(2,1)} %down.1), custom_call_target="tpu_custom_call" | custom-call | tf_op jit(solution)/shard_map/stage/pallas_call | solution.py:96
  5.1 0.6 collective-permute-start.7
  5.6 0.1 collective-permute-start.8
  5.7 1.0 %pack.1.refs_0_ = bf16[64,2176]{1,0:T(8,128)(2,1)S(1)} custom-call(bf16[64,2048]{1,0:T(8,128)(2,1)} %tokens.1, bf16[8,64]{1,0:T(8,128)(2,1)} %bitcast.19, s32[8,64]{1,0:T(8,128)} %bitcast.17, s32[8,64]{1,0:T(8,128)} %bitcast.18), custom_call_target="tpu_custom_call" | custom-call | tf_op jit(solution)/shard_map/pack/pallas_call | solution.py:64
  6.7 2.7 %collective-permute-start = (bf16[64,2176]{1,0:T(8,128)(2,1)S(1)}, bf16[64,2176]{1,0:T(8,128)(2,1)S(1)}, u32[]{:S(2)}, u32[]{:S(2)}) collective-permute-start(bf16[64,2176]{1,0:T(8,128)(2,1)S(1)} %pack.1.refs_0_), channel_id=1, source_target_pairs={{0,5},{4,1},{5,8},{9,4},{8,13},{12,9},{13,14},{15,12},{14,11},{10,... | collective-permute-start | bytes 835592 | tf_op jit(solution)/shard_map/ppermute | solution.py:208
  9.5 1.5 %collective-permute-start.3 = (bf16[64,2176]{1,0:T(8,128)(2,1)S(1)}, bf16[64,2176]{1,0:T(8,128)(2,1)S(1)}, u32[]{:S(2)}, u32[]{:S(2)}) collective-permute-start(bf16[64,2176]{1,0:T(8,128)(2,1)S(1)} %pack.1.refs_0_), channel_id=1, source_target_pairs={{1,5},{5,1},{4,8},{8,4},{9,13},{13,9},{12,14},{14,12},{15,11},{11,... | collective-permute-start | bytes 835592 | tf_op jit(solution)/shard_map/ppermute | solution.py:209
  11.0 4.5 %collective-permute-done.refs_1_ = bf16[64,2176]{1,0:T(8,128)(2,1)S(1)} collective-permute-done((bf16[64,2176]{1,0:T(8,128)(2,1)S(1)}, bf16[64,2176]{1,0:T(8,128)(2,1)S(1)}, u32[]{:S(2)}, u32[]{:S(2)}) %collective-permute-start) | collective-permute-done | bytes 278560 | tf_op jit(solution)/shard_map/ppermute | solution.py:208
  15.5 2.2 %collective-permute-start.1 = (bf16[64,2176]{1,0:T(8,128)(2,1)S(1)}, bf16[64,2176]{1,0:T(8,128)(2,1)S(1)}, u32[]{:S(2)}, u32[]{:S(2)}) collective-permute-start(bf16[64,2176]{1,0:T(8,128)(2,1)S(1)} %collective-permute-done.refs_1_), channel_id=1, source_target_pairs={{0,5},{4,1},{5,8},{9,4},{8,13},{12,9},{13,14},{15,12},{14,11},{10,... | collective-permute-start | bytes 835592 | tf_op jit(solution)/shard_map/ppermute | solution.py:215
  17.7 0.0 collective-permute-done.3.refs_2_
  17.7 0.8 %collective-permute-start.4 = (bf16[64,2176]{1,0:T(8,128)(2,1)S(1)}, bf16[64,2176]{1,0:T(8,128)(2,1)S(1)}, u32[]{:S(2)}, u32[]{:S(2)}) collective-permute-start(bf16[64,2176]{1,0:T(8,128)(2,1)S(1)} %collective-permute-done.3.refs_2_), channel_id=1, source_target_pairs={{0,5},{4,1},{5,8},{9,4},{8,13},{12,9},{13,14},{15,12},{14,11},{10,... | collective-permute-start | bytes 835592 | tf_op jit(solution)/shard_map/ppermute | solution.py:217
  18.5 3.6 %collective-permute-done.1.refs_3_ = bf16[64,2176]{1,0:T(8,128)(2,1)S(1)} collective-permute-done((bf16[64,2176]{1,0:T(8,128)(2,1)S(1)}, bf16[64,2176]{1,0:T(8,128)(2,1)S(1)}, u32[]{:S(2)}, u32[]{:S(2)}) %collective-permute-start.1) | collective-permute-done | bytes 278560 | tf_op jit(solution)/shard_map/ppermute | solution.py:215
  22.0 1.9 %collective-permute-start.2 = (bf16[64,2176]{1,0:T(8,128)(2,1)S(1)}, bf16[64,2176]{1,0:T(8,128)(2,1)S(1)}, u32[]{:S(2)}, u32[]{:S(2)}) collective-permute-start(bf16[64,2176]{1,0:T(8,128)(2,1)S(1)} %collective-permute-done.1.refs_3_), channel_id=1, source_target_pairs={{0,5},{4,1},{5,8},{9,4},{8,13},{12,9},{13,14},{15,12},{14,11},{10,... | collective-permute-start | bytes 835592 | tf_op jit(solution)/shard_map/ppermute | solution.py:215
  23.9 1.1 %collective-permute-done.4.refs_4_ = bf16[64,2176]{1,0:T(8,128)(2,1)S(1)} collective-permute-done((bf16[64,2176]{1,0:T(8,128)(2,1)S(1)}, bf16[64,2176]{1,0:T(8,128)(2,1)S(1)}, u32[]{:S(2)}, u32[]{:S(2)}) %collective-permute-start.4) | collective-permute-done | bytes 278560 | tf_op jit(solution)/shard_map/ppermute | solution.py:217
  25.0 1.9 %collective-permute-start.5 = (bf16[64,2176]{1,0:T(8,128)(2,1)S(1)}, bf16[64,2176]{1,0:T(8,128)(2,1)S(1)}, u32[]{:S(2)}, u32[]{:S(2)}) collective-permute-start(bf16[64,2176]{1,0:T(8,128)(2,1)S(1)} %collective-permute-done.4.refs_4_), channel_id=1, source_target_pairs={{0,5},{4,1},{5,8},{9,4},{8,13},{12,9},{13,14},{15,12},{14,11},{10,... | collective-permute-start | bytes 835592 | tf_op jit(solution)/shard_map/ppermute | solution.py:217
  26.9 1.4 %collective-permute-done.2.refs_0_ = bf16[64,2176]{1,0:T(8,128)(2,1)S(1)} collective-permute-done((bf16[64,2176]{1,0:T(8,128)(2,1)S(1)}, bf16[64,2176]{1,0:T(8,128)(2,1)S(1)}, u32[]{:S(2)}, u32[]{:S(2)}) %collective-permute-start.2) | collective-permute-done | bytes 278560 | tf_op jit(solution)/shard_map/ppermute | solution.py:215
  28.3 1.9 %collective-permute-start.6 = (bf16[64,2176]{1,0:T(8,128)(2,1)S(1)}, bf16[64,2176]{1,0:T(8,128)(2,1)S(1)}, u32[]{:S(2)}, u32[]{:S(2)}) collective-permute-start(bf16[64,2176]{1,0:T(8,128)(2,1)S(1)} %collective-permute-done.2.refs_0_), channel_id=1, source_target_pairs={{0,5},{4,1},{5,8},{9,4},{8,13},{12,9},{13,14},{15,12},{14,11},{10,... | collective-permute-start | bytes 835592 | tf_op jit(solution)/shard_map/ppermute | solution.py:215
  30.2 1.1 %collective-permute-done.5.refs_1_ = bf16[64,2176]{1,0:T(8,128)(2,1)S(1)} collective-permute-done((bf16[64,2176]{1,0:T(8,128)(2,1)S(1)}, bf16[64,2176]{1,0:T(8,128)(2,1)S(1)}, u32[]{:S(2)}, u32[]{:S(2)}) %collective-permute-start.5) | collective-permute-done | bytes 278560 | tf_op jit(solution)/shard_map/ppermute | solution.py:217
  31.3 3.3 %collective-permute-done.6.refs_2_ = bf16[64,2176]{1,0:T(8,128)(2,1)S(1)} collective-permute-done((bf16[64,2176]{1,0:T(8,128)(2,1)S(1)}, bf16[64,2176]{1,0:T(8,128)(2,1)S(1)}, u32[]{:S(2)}, u32[]{:S(2)}) %collective-permute-start.6) | collective-permute-done | bytes 278560 | tf_op jit(solution)/shard_map/ppermute | solution.py:215
  34.6 0.0 collective-permute-done.8.refs_6_
  34.6 0.0 collective-permute-done.7.refs_5_
  34.6 4.7 %expert.3 = (bf16[64,2048]{1,0:T(8,128)(2,1)S(1)}, bf16[64,2048]{1,0:T(8,128)(2,1)S(1)}, bf16[64,2048]{1,0:T(8,128)(2,1)S(1)}) custom-call(s32[2]{0:T(128)S(1)} %pad_add_fusion.first_ref, bf16[64,2176]{1,0:T(8,128)(2,1)S(1)} %collective-permute-done.2.refs_0_, bf16[64,2176]{1,0:T(8,128)(2,1)S(1)} %collective-permute-done.5.refs_1_, ...), custom_call_target="tpu_custom_call" | custom-call | tf_op jit(solution)/shard_map/expert/pallas_call | solution.py:155
  39.3 1.8 %collective-permute-start.9 = (bf16[64,2048]{1,0:T(8,128)(2,1)S(1)}, bf16[64,2048]{1,0:T(8,128)(2,1)S(1)}, u32[]{:S(2)}, u32[]{:S(2)}) collective-permute-start(bf16[64,2048]{1,0:T(8,128)(2,1)S(1)} %get-tuple-element.21), channel_id=1, source_target_pairs={{5,0},{1,4},{8,5},{4,9},{13,8},{9,12},{14,13},{12,15},{11,14},{15,... | collective-permute-start | bytes 786440 | tf_op jit(solution)/shard_map/ppermute | solution.py:241
  41.1 4.1 %expert.4 = (f32[64,2048]{1,0:T(8,128)S(1)}, f32[64,2048]{1,0:T(8,128)S(1)}, f32[64,2048]{1,0:T(8,128)S(1)}, f32[64,2048]{1,0:T(8,128)S(1)}, f32[64,2048]{1,0:T(8,128)S(1)}) custom-call(s32[2]{0:T(128)S(1)} %pad_add_fusion.first_ref, bf16[64,2176]{1,0:T(8,128)(2,1)S(1)} %pack.1.refs_0_, bf16[64,2176]{1,0:T(8,128)(2,1)S(1)} %collective-permute-done.refs_1_, ...), custom_call_target="tpu_custom_call" | custom-call | tf_op jit(solution)/shard_map/expert/pallas_call | solution.py:155
  45.2 1.8 %collective-permute-start.13 = (bf16[64,2048]{1,0:T(8,128)(2,1)S(1)}, bf16[64,2048]{1,0:T(8,128)(2,1)S(1)}, u32[]{:S(2)}, u32[]{:S(2)}) collective-permute-start(bf16[64,2048]{1,0:T(8,128)(2,1)S(1)} %get-tuple-element.31), channel_id=1, source_target_pairs={{5,0},{1,4},{8,5},{4,9},{13,8},{9,12},{14,13},{12,15},{11,14},{15,... | collective-permute-start | bytes 786440 | tf_op jit(solution)/shard_map/ppermute | solution.py:244
  47.0 4.1 %expert.5 = (bf16[64,2048]{1,0:T(8,128)(2,1)S(1)}, bf16[64,2048]{1,0:T(8,128)(2,1)S(1)}, bf16[64,2048]{1,0:T(8,128)(2,1)S(1)}, bf16[64,2048]{1,0:T(8,128)(2,1)S(1)}, bf16[64,2048]{1,0:T(8,128)(2,1)S(1)}) custom-call(s32[2]{0:T(128)S(1)} %pad_add_fusion.first_ref, bf16[64,2176]{1,0:T(8,128)(2,1)S(1)} %pack.1.refs_0_, ...), custom_call_target="tpu_custom_call" | custom-call | tf_op jit(solution)/shard_map/expert/pallas_call | solution.py:155
  51.1 0.0 collective-permute-done.9
  51.1 0.1 add_convert_fusion.5
  51.2 1.8 %collective-permute-start.10 = (bf16[64,2048]{1,0:T(8,128)(2,1)S(1)}, bf16[64,2048]{1,0:T(8,128)(2,1)S(1)}, u32[]{:S(2)}, u32[]{:S(2)}) collective-permute-start(bf16[64,2048]{1,0:T(8,128)(2,1)S(1)} %add_convert_fusion.5), channel_id=1, source_target_pairs={{5,0},{1,4},{8,5},{4,9},{13,8},{9,12},{14,13},{12,15},{11,14},{15,... | collective-permute-start | bytes 786440 | tf_op jit(solution)/shard_map/ppermute | solution.py:241
  53.0 0.0 collective-permute-done.13
  53.0 0.1 add_convert_fusion.2
  53.0 0.0 copy-start.1
  53.0 0.0 copy-start.2
  53.1 0.3 collective-permute-start.14
  53.4 3.6 %collective-permute-done.10 = bf16[64,2048]{1,0:T(8,128)(2,1)S(1)} collective-permute-done((bf16[64,2048]{1,0:T(8,128)(2,1)S(1)}, bf16[64,2048]{1,0:T(8,128)(2,1)S(1)}, u32[]{:S(2)}, u32[]{:S(2)}) %collective-permute-start.10) | collective-permute-done | bytes 262176 | tf_op jit(solution)/shard_map/ppermute | solution.py:241
  57.0 0.1 add_convert_fusion.4
  57.1 2.1 %collective-permute-start.11 = (bf16[64,2048]{1,0:T(8,128)(2,1)S(1)}, bf16[64,2048]{1,0:T(8,128)(2,1)S(1)}, u32[]{:S(2)}, u32[]{:S(2)}) collective-permute-start(bf16[64,2048]{1,0:T(8,128)(2,1)S(1)} %add_convert_fusion.4), channel_id=1, source_target_pairs={{5,0},{1,4},{8,5},{4,9},{13,8},{9,12},{14,13},{12,15},{11,14},{15,... | collective-permute-start | bytes 786440 | tf_op jit(solution)/shard_map/ppermute | solution.py:241
  59.2 0.6 collective-permute-done.14
  59.8 0.1 add_convert_fusion.1
  59.9 0.1 collective-permute-start.15
  60.0 3.1 %collective-permute-done.11 = bf16[64,2048]{1,0:T(8,128)(2,1)S(1)} collective-permute-done((bf16[64,2048]{1,0:T(8,128)(2,1)S(1)}, bf16[64,2048]{1,0:T(8,128)(2,1)S(1)}, u32[]{:S(2)}, u32[]{:S(2)}) %collective-permute-start.11) | collective-permute-done | bytes 262176 | tf_op jit(solution)/shard_map/ppermute | solution.py:241
  63.1 0.1 add_convert_fusion.3
  63.1 0.0 copy-done.1
  63.1 0.1 iota_compare_fusion
  63.2 1.9 %collective-permute-start.12 = (bf16[64,2048]{1,0:T(8,128)(2,1)S(1)}, bf16[64,2048]{1,0:T(8,128)(2,1)S(1)}, u32[]{:S(2)}, u32[]{:S(2)}) collective-permute-start(bf16[64,2048]{1,0:T(8,128)(2,1)S(1)} %add_convert_fusion.3), channel_id=1, source_target_pairs={{5,0},{1,4},{8,5},{4,9},{13,8},{9,12},{14,13},{12,15},{11,14},{15,... | collective-permute-start | bytes 786440 | tf_op jit(solution)/shard_map/ppermute | solution.py:247
  65.1 0.0 copy-done
  65.1 0.0 copy-done.2
  65.1 0.7 fusion.22
  65.8 1.7 %fusion.17 = bf16[1,2,32,128]{3,2,1,0:T(8,128)(2,1)S(1)} fusion(bf16[2,640,4,128]{3,2,1,0:T(4,128)(2,1)} %param.20, f32[2,4,8,640]{3,2,1,0:T(8,128)S(1)} %get-tuple-element.37, f32[2,4,8]{2,1,0:T(4,128)S(1)} %get-tuple-element.36), kind=kOutput, calls=%fused_computation.11 | convolution fusion | flops 10575872 | bytes 1491200 | tf_op jit(solution)/shard_map/rkgl,rlkd->rkgd/dot_general | solution.py:31
  67.5 0.6 copy.31
  68.1 0.0 collective-permute-done.15
  68.2 0.9 %collective-permute-done.12 = bf16[64,2048]{1,0:T(8,128)(2,1)S(1)} collective-permute-done((bf16[64,2048]{1,0:T(8,128)(2,1)S(1)}, bf16[64,2048]{1,0:T(8,128)(2,1)S(1)}, u32[]{:S(2)}, u32[]{:S(2)}) %collective-permute-start.12) | collective-permute-done | bytes 262176 | tf_op jit(solution)/shard_map/ppermute | solution.py:247
  69.0 0.8 %add_convert_fusion = bf16[64,2048]{1,0:T(8,128)(2,1)} fusion(bf16[64,2048]{1,0:T(8,128)(2,1)S(1)} %get-tuple-element.34, bf16[64,2048]{1,0:T(8,128)(2,1)S(1)} %collective-permute-done.15, bf16[64,2048]{1,0:T(8,128)(2,1)S(1)} %collective-permute-done.12), kind=kLoop, calls=%fused_computation.12 | loop fusion | flops 786432 | bytes 1048576 | tf_op jit(solution)/shard_map/convert_element_type | solution.py:255
Async XLA Ops:
  0.6 64.5 %copy-start = (bf16[2,640,4,128]{3,2,1,0:T(4,128)(2,1)S(1)}, bf16[2,640,4,128]{3,2,1,0:T(4,128)(2,1)}, u32[]{:S(2)}) copy-start(bf16[2,640,4,128]{3,2,1,0:T(4,128)(2,1)} %param.19) | copy-start | bytes 3932164
  5.1 29.5 %collective-permute-start.7 = (bf16[2,2048,768]{2,1,0:T(8,128)(2,1)S(1)}, bf16[2,2048,768]{2,1,0:T(8,128)(2,1)S(1)}, u32[]{:S(2)}, u32[]{:S(2)}) collective-permute-start(bf16[2,2048,768]{2,1,0:T(8,128)(2,1)S(1)} %get-tuple-element.19.refs_3_.refs_5_), channel_id=1, source_target_pairs={{0,1},{1,0},{2,3},{3,2},{4,5},{5,4},{6,7},{7,6},{8,9},{9,8},{10,11... | collective-permute-start | bytes 18874376 | tf_op jit(solution)/shard_map/ppermute | solution.py:213
  5.6 28.9 %collective-permute-start.8 = (bf16[2,384,2048]{2,1,0:T(8,128)(2,1)S(1)}, bf16[2,384,2048]{2,1,0:T(8,128)(2,1)S(1)}, u32[]{:S(2)}, u32[]{:S(2)}) collective-permute-start(bf16[2,384,2048]{2,1,0:T(8,128)(2,1)S(1)} %get-tuple-element.20.refs_4_.refs_6_), channel_id=1, source_target_pairs={{0,1},{1,0},{2,3},{3,2},{4,5},{5,4},{6,7},{7,6},{8,9},{9,8},{10,11... | collective-permute-start | bytes 9437192 | tf_op jit(solution)/shard_map/ppermute | solution.py:213
  6.7 8.7 %collective-permute-start = (bf16[64,2176]{1,0:T(8,128)(2,1)S(1)}, bf16[64,2176]{1,0:T(8,128)(2,1)S(1)}, u32[]{:S(2)}, u32[]{:S(2)}) collective-permute-start(bf16[64,2176]{1,0:T(8,128)(2,1)S(1)} %pack.1.refs_0_), channel_id=1, source_target_pairs={{0,5},{4,1},{5,8},{9,4},{8,13},{12,9},{13,14},{15,12},{14,11},{10,... | collective-permute-start | bytes 835592 | tf_op jit(solution)/shard_map/ppermute | solution.py:208
  9.5 8.2 %collective-permute-start.3 = (bf16[64,2176]{1,0:T(8,128)(2,1)S(1)}, bf16[64,2176]{1,0:T(8,128)(2,1)S(1)}, u32[]{:S(2)}, u32[]{:S(2)}) collective-permute-start(bf16[64,2176]{1,0:T(8,128)(2,1)S(1)} %pack.1.refs_0_), channel_id=1, source_target_pairs={{1,5},{5,1},{4,8},{8,4},{9,13},{13,9},{12,14},{14,12},{15,11},{11,... | collective-permute-start | bytes 835592 | tf_op jit(solution)/shard_map/ppermute | solution.py:209
  15.5 6.5 %collective-permute-start.1 = (bf16[64,2176]{1,0:T(8,128)(2,1)S(1)}, bf16[64,2176]{1,0:T(8,128)(2,1)S(1)}, u32[]{:S(2)}, u32[]{:S(2)}) collective-permute-start(bf16[64,2176]{1,0:T(8,128)(2,1)S(1)} %collective-permute-done.refs_1_), channel_id=1, source_target_pairs={{0,5},{4,1},{5,8},{9,4},{8,13},{12,9},{13,14},{15,12},{14,11},{10,... | collective-permute-start | bytes 835592 | tf_op jit(solution)/shard_map/ppermute | solution.py:215
  17.7 7.3 %collective-permute-start.4 = (bf16[64,2176]{1,0:T(8,128)(2,1)S(1)}, bf16[64,2176]{1,0:T(8,128)(2,1)S(1)}, u32[]{:S(2)}, u32[]{:S(2)}) collective-permute-start(bf16[64,2176]{1,0:T(8,128)(2,1)S(1)} %collective-permute-done.3.refs_2_), channel_id=1, source_target_pairs={{0,5},{4,1},{5,8},{9,4},{8,13},{12,9},{13,14},{15,12},{14,11},{10,... | collective-permute-start | bytes 835592 | tf_op jit(solution)/shard_map/ppermute | solution.py:217
  22.0 6.3 %collective-permute-start.2 = (bf16[64,2176]{1,0:T(8,128)(2,1)S(1)}, bf16[64,2176]{1,0:T(8,128)(2,1)S(1)}, u32[]{:S(2)}, u32[]{:S(2)}) collective-permute-start(bf16[64,2176]{1,0:T(8,128)(2,1)S(1)} %collective-permute-done.1.refs_3_), channel_id=1, source_target_pairs={{0,5},{4,1},{5,8},{9,4},{8,13},{12,9},{13,14},{15,12},{14,11},{10,... | collective-permute-start | bytes 835592 | tf_op jit(solution)/shard_map/ppermute | solution.py:215
  25.0 6.3 %collective-permute-start.5 = (bf16[64,2176]{1,0:T(8,128)(2,1)S(1)}, bf16[64,2176]{1,0:T(8,128)(2,1)S(1)}, u32[]{:S(2)}, u32[]{:S(2)}) collective-permute-start(bf16[64,2176]{1,0:T(8,128)(2,1)S(1)} %collective-permute-done.4.refs_4_), channel_id=1, source_target_pairs={{0,5},{4,1},{5,8},{9,4},{8,13},{12,9},{13,14},{15,12},{14,11},{10,... | collective-permute-start | bytes 835592 | tf_op jit(solution)/shard_map/ppermute | solution.py:217
  28.3 6.3 %collective-permute-start.6 = (bf16[64,2176]{1,0:T(8,128)(2,1)S(1)}, bf16[64,2176]{1,0:T(8,128)(2,1)S(1)}, u32[]{:S(2)}, u32[]{:S(2)}) collective-permute-start(bf16[64,2176]{1,0:T(8,128)(2,1)S(1)} %collective-permute-done.2.refs_0_), channel_id=1, source_target_pairs={{0,5},{4,1},{5,8},{9,4},{8,13},{12,9},{13,14},{15,12},{14,11},{10,... | collective-permute-start | bytes 835592 | tf_op jit(solution)/shard_map/ppermute | solution.py:215
  39.3 11.8 %collective-permute-start.9 = (bf16[64,2048]{1,0:T(8,128)(2,1)S(1)}, bf16[64,2048]{1,0:T(8,128)(2,1)S(1)}, u32[]{:S(2)}, u32[]{:S(2)}) collective-permute-start(bf16[64,2048]{1,0:T(8,128)(2,1)S(1)} %get-tuple-element.21), channel_id=1, source_target_pairs={{5,0},{1,4},{8,5},{4,9},{13,8},{9,12},{14,13},{12,15},{11,14},{15,... | collective-permute-start | bytes 786440 | tf_op jit(solution)/shard_map/ppermute | solution.py:241
  45.2 7.8 %collective-permute-start.13 = (bf16[64,2048]{1,0:T(8,128)(2,1)S(1)}, bf16[64,2048]{1,0:T(8,128)(2,1)S(1)}, u32[]{:S(2)}, u32[]{:S(2)}) collective-permute-start(bf16[64,2048]{1,0:T(8,128)(2,1)S(1)} %get-tuple-element.31), channel_id=1, source_target_pairs={{5,0},{1,4},{8,5},{4,9},{13,8},{9,12},{14,13},{12,15},{11,14},{15,... | collective-permute-start | bytes 786440 | tf_op jit(solution)/shard_map/ppermute | solution.py:244
  51.2 5.8 %collective-permute-start.10 = (bf16[64,2048]{1,0:T(8,128)(2,1)S(1)}, bf16[64,2048]{1,0:T(8,128)(2,1)S(1)}, u32[]{:S(2)}, u32[]{:S(2)}) collective-permute-start(bf16[64,2048]{1,0:T(8,128)(2,1)S(1)} %add_convert_fusion.5), channel_id=1, source_target_pairs={{5,0},{1,4},{8,5},{4,9},{13,8},{9,12},{14,13},{12,15},{11,14},{15,... | collective-permute-start | bytes 786440 | tf_op jit(solution)/shard_map/ppermute | solution.py:241
  53.0 10.1 %copy-start.1 = (s32[2]{0:T(128)S(1)}, s32[2]{0:T(128)}, u32[]{:S(2)}) copy-start(s32[2]{0:T(128)} %param.21) | copy-start | bytes 28
  53.0 12.1 %copy-start.2 = (bf16[2,32,128]{2,1,0:T(8,128)(2,1)S(1)}, bf16[2,32,128]{2,1,0:T(8,128)(2,1)}, u32[]{:S(2)}) copy-start(bf16[2,32,128]{2,1,0:T(8,128)(2,1)} %param.18) | copy-start | bytes 49156
  53.1 6.8 %collective-permute-start.14 = (bf16[64,2048]{1,0:T(8,128)(2,1)S(1)}, bf16[64,2048]{1,0:T(8,128)(2,1)S(1)}, u32[]{:S(2)}, u32[]{:S(2)}) collective-permute-start(bf16[64,2048]{1,0:T(8,128)(2,1)S(1)} %add_convert_fusion.2), channel_id=1, source_target_pairs={{5,0},{1,4},{8,5},{4,9},{13,8},{9,12},{14,13},{12,15},{11,14},{15,... | collective-permute-start | bytes 786440 | tf_op jit(solution)/shard_map/ppermute | solution.py:244
  57.1 6.0 %collective-permute-start.11 = (bf16[64,2048]{1,0:T(8,128)(2,1)S(1)}, bf16[64,2048]{1,0:T(8,128)(2,1)S(1)}, u32[]{:S(2)}, u32[]{:S(2)}) collective-permute-start(bf16[64,2048]{1,0:T(8,128)(2,1)S(1)} %add_convert_fusion.4), channel_id=1, source_target_pairs={{5,0},{1,4},{8,5},{4,9},{13,8},{9,12},{14,13},{12,15},{11,14},{15,... | collective-permute-start | bytes 786440 | tf_op jit(solution)/shard_map/ppermute | solution.py:241
  59.9 8.3 %collective-permute-start.15 = (bf16[64,2048]{1,0:T(8,128)(2,1)S(1)}, bf16[64,2048]{1,0:T(8,128)(2,1)S(1)}, u32[]{:S(2)}, u32[]{:S(2)}) collective-permute-start(bf16[64,2048]{1,0:T(8,128)(2,1)S(1)} %add_convert_fusion.1), channel_id=1, source_target_pairs={{5,1},{1,5},{8,4},{4,8},{13,9},{9,13},{14,12},{12,14},{11,15},{15,... | collective-permute-start | bytes 786440 | tf_op jit(solution)/shard_map/ppermute | solution.py:248
  63.2 5.8 %collective-permute-start.12 = (bf16[64,2048]{1,0:T(8,128)(2,1)S(1)}, bf16[64,2048]{1,0:T(8,128)(2,1)S(1)}, u32[]{:S(2)}, u32[]{:S(2)}) collective-permute-start(bf16[64,2048]{1,0:T(8,128)(2,1)S(1)} %add_convert_fusion.3), channel_id=1, source_target_pairs={{5,0},{1,4},{8,5},{4,9},{13,8},{9,12},{14,13},{12,15},{11,14},{15,... | collective-permute-start | bytes 786440 | tf_op jit(solution)/shard_map/ppermute | solution.py:247

commit v3 on v2

--- a/solution.py
+++ b/solution.py
@@ -215,25 +215,19 @@
         near_rows[k] = lax.ppermute(near_rows[k - 1], AXES, same)
         if k < far:
             far_rows[k] = lax.ppermute(far_rows[k - 1], AXES, same)
+    rows_of = {("own", 0): own}
+    rows_of.update({("near", k): v for k, v in near_rows.items()})
+    rows_of.update({("far", k): v for k, v in far_rows.items()})
     partial = {}
     for group in groups_of(far):
-        names, blocks = [], []
-        for k in group:
-            if k == 0:
-                names.append(("own", 0))
-                blocks.append(own)
-                continue
-            names.append(("near", k))
-            blocks.append(near_rows[k])
-            if k < far:
-                names.append(("far", k))
-                blocks.append(far_rows[k])
+        names = [n for k in group for n in names_of(k, far)]
         top = group[-1]
         if top == far:
-            outs = expert(blocks, mine + theirs, 0, first, [], jnp.bfloat16)
-        else:
-            sums = expert(blocks, mine, 0, first, [], jnp.float32)
-            outs = expert(blocks, theirs, 1, first, sums, jnp.bfloat16)
+            outs = expert([rows_of[n] for n in names], mine + theirs, 0, first, [], jnp.bfloat16)
+            partial.update(zip(names, outs, strict=True))
+            continue
+        outs = expert([rows_of[n] for n in names], mine, 0, first, [], jnp.float32)
+        outs = expert([rows_of[n] for n in names], theirs, 1, first, list(outs), jnp.bfloat16)
         partial.update(zip(names, outs, strict=True))
     near_sum = partial["near", far]
     far_sum = partial["far", far - 1]
@@ -256,12 +250,14 @@
 
 
 def groups_of(far):
-    groups = []
-    while far > 2:
-        groups.append([far - 1, far])
-        far -= 2
-    groups.append(list(range(far + 1)))
-    return groups[::-1]
+    near = [list(range(k, min(k + 2, far - 2))) for k in range(0, far - 2, 2)]
+    return [*near, [far - 2], [far - 1, far]]
+
+
+def names_of(k, far):
+    if k == 0:
+        return [("own", 0)]
+    return [("near", k), ("far", k)] if k < far else [("near", k)]
 
 
 def solution(mesh):

time: 70 us -> 71.8 us (1.026)
  Pallas kernels: 18.3 us -> 20.1 us
    pallas_call x3 -> x5, Pallas kernels: 12.9 us -> 14.7 us  [expert(): pl.pallas_call(functools.partial(expert_kernel, count, sources, base, boo...]
  transfers between devices with their start and end apart: 16 -> 16, of which waited for: 10 -> 10; matrix products, arithmetic and copies ran while one was open for 5% -> 5% of each run, Pallas kernels for 13% -> 15%
where the time goes in v3:
time: 71.8 us; the launch traced here: 71.6 us
  starting transfers between devices  23.5 us (33%)
  waiting for transfers between devices  23 us (32%)
  Pallas kernels  20.1 us (28%)
  matrix products  2.38 us (3%)
  other arithmetic  1.28 us (2%)
  between operations  0.78 us (1%)
    pallas_call x5, Pallas kernels, expert(): pl.pallas_call(functools.partial(expert_kernel, count, sources, base, boo...  14.7 us
    ppermute x3, waiting for transfers between devices, local(): near_rows[k] = lax.ppermute(near_rows[k - 1], AXES, same)  8.19 us
    ppermute x4, starting transfers between devices, local(): near_sum = lax.ppermute(near_sum, AXES, same_back)  7.63 us
    ppermute x4, waiting for transfers between devices, local(): near_sum = lax.ppermute(near_sum, AXES, same_back)  7.51 us
    ppermute x3, starting transfers between devices, local(): near_rows[k] = lax.ppermute(near_rows[k - 1], AXES, same)  6.06 us
    ppermute x1, waiting for transfers between devices, local(): near_rows[1] = lax.ppermute(own, AXES, same)  4.49 us
    pallas_call x1, Pallas kernels, stage(): pl.pallas_call(stage_kernel, out_shape=[pltpu.VMEM((slots, width, 2 * hal...  4.33 us
    ppermute x1, starting transfers between devices, local(): near_rows[1] = lax.ppermute(own, AXES, same)  2.73 us
  transfers between devices with their start and end apart: 16, of which 10 were waited for; matrix products, arithmetic and copies ran while one was open for 5% of the time, Pallas kernels for 15%

profile of v3, /device:TPU:0, one launch (start us, length us, event | category | flops | bytes accessed | tf_op | source)
XLA Modules:
  0.0 71.6 jit_solution(5689130102087397758)
XLA Ops:
  0.6 0.0 copy-start
  0.7 0.1 pad_add_fusion.first_ref
  0.7 4.3 %stage.1 = (bf16[2,2048,768]{2,1,0:T(8,128)(2,1)S(1)}, bf16[2,384,2048]{2,1,0:T(8,128)(2,1)S(1)}) custom-call(s32[2]{0:T(128)S(1)} %pad_add_fusion.first_ref, bf16[2,2048,384]{2,1,0:T(8,128)(2,1)} %gate.1, bf16[2,2048,384]{2,1,0:T(8,128)(2,1)} %up.1, bf16[2,384,2048]{2,1,0:T(8,128)(2,1)} %down.1), custom_call_target="tpu_custom_call" | custom-call | tf_op jit(solution)/shard_map/stage/pallas_call | solution.py:96
  5.1 0.6 collective-permute-start.7
  5.6 0.1 collective-permute-start.8
  5.7 1.0 %pack.1.refs_0_ = bf16[64,2176]{1,0:T(8,128)(2,1)S(1)} custom-call(bf16[64,2048]{1,0:T(8,128)(2,1)} %tokens.1, bf16[8,64]{1,0:T(8,128)(2,1)} %bitcast.19, s32[8,64]{1,0:T(8,128)} %bitcast.17, s32[8,64]{1,0:T(8,128)} %bitcast.18), custom_call_target="tpu_custom_call" | custom-call | tf_op jit(solution)/shard_map/pack/pallas_call | solution.py:64
  6.7 2.7 %collective-permute-start = (bf16[64,2176]{1,0:T(8,128)(2,1)S(1)}, bf16[64,2176]{1,0:T(8,128)(2,1)S(1)}, u32[]{:S(2)}, u32[]{:S(2)}) collective-permute-start(bf16[64,2176]{1,0:T(8,128)(2,1)S(1)} %pack.1.refs_0_), channel_id=1, source_target_pairs={{0,5},{4,1},{5,8},{9,4},{8,13},{12,9},{13,14},{15,12},{14,11},{10,... | collective-permute-start | bytes 835592 | tf_op jit(solution)/shard_map/ppermute | solution.py:208
  9.5 1.5 %collective-permute-start.3 = (bf16[64,2176]{1,0:T(8,128)(2,1)S(1)}, bf16[64,2176]{1,0:T(8,128)(2,1)S(1)}, u32[]{:S(2)}, u32[]{:S(2)}) collective-permute-start(bf16[64,2176]{1,0:T(8,128)(2,1)S(1)} %pack.1.refs_0_), channel_id=1, source_target_pairs={{1,5},{5,1},{4,8},{8,4},{9,13},{13,9},{12,14},{14,12},{15,11},{11,... | collective-permute-start | bytes 835592 | tf_op jit(solution)/shard_map/ppermute | solution.py:209
  11.0 4.5 %collective-permute-done.refs_1_ = bf16[64,2176]{1,0:T(8,128)(2,1)S(1)} collective-permute-done((bf16[64,2176]{1,0:T(8,128)(2,1)S(1)}, bf16[64,2176]{1,0:T(8,128)(2,1)S(1)}, u32[]{:S(2)}, u32[]{:S(2)}) %collective-permute-start) | collective-permute-done | bytes 278560 | tf_op jit(solution)/shard_map/ppermute | solution.py:208
  15.5 2.2 %collective-permute-start.1 = (bf16[64,2176]{1,0:T(8,128)(2,1)S(1)}, bf16[64,2176]{1,0:T(8,128)(2,1)S(1)}, u32[]{:S(2)}, u32[]{:S(2)}) collective-permute-start(bf16[64,2176]{1,0:T(8,128)(2,1)S(1)} %collective-permute-done.refs_1_), channel_id=1, source_target_pairs={{0,5},{4,1},{5,8},{9,4},{8,13},{12,9},{13,14},{15,12},{14,11},{10,... | collective-permute-start | bytes 835592 | tf_op jit(solution)/shard_map/ppermute | solution.py:215
  17.7 0.0 collective-permute-done.3.refs_2_
  17.7 0.8 %collective-permute-start.4 = (bf16[64,2176]{1,0:T(8,128)(2,1)S(1)}, bf16[64,2176]{1,0:T(8,128)(2,1)S(1)}, u32[]{:S(2)}, u32[]{:S(2)}) collective-permute-start(bf16[64,2176]{1,0:T(8,128)(2,1)S(1)} %collective-permute-done.3.refs_2_), channel_id=1, source_target_pairs={{0,5},{4,1},{5,8},{9,4},{8,13},{12,9},{13,14},{15,12},{14,11},{10,... | collective-permute-start | bytes 835592 | tf_op jit(solution)/shard_map/ppermute | solution.py:217
  18.5 3.6 %collective-permute-done.1.refs_0_ = bf16[64,2176]{1,0:T(8,128)(2,1)S(1)} collective-permute-done((bf16[64,2176]{1,0:T(8,128)(2,1)S(1)}, bf16[64,2176]{1,0:T(8,128)(2,1)S(1)}, u32[]{:S(2)}, u32[]{:S(2)}) %collective-permute-start.1) | collective-permute-done | bytes 278560 | tf_op jit(solution)/shard_map/ppermute | solution.py:215
  22.0 1.9 %collective-permute-start.2 = (bf16[64,2176]{1,0:T(8,128)(2,1)S(1)}, bf16[64,2176]{1,0:T(8,128)(2,1)S(1)}, u32[]{:S(2)}, u32[]{:S(2)}) collective-permute-start(bf16[64,2176]{1,0:T(8,128)(2,1)S(1)} %collective-permute-done.1.refs_0_), channel_id=1, source_target_pairs={{0,5},{4,1},{5,8},{9,4},{8,13},{12,9},{13,14},{15,12},{14,11},{10,... | collective-permute-start | bytes 835592 | tf_op jit(solution)/shard_map/ppermute | solution.py:215
  23.9 1.1 %collective-permute-done.4.refs_1_ = bf16[64,2176]{1,0:T(8,128)(2,1)S(1)} collective-permute-done((bf16[64,2176]{1,0:T(8,128)(2,1)S(1)}, bf16[64,2176]{1,0:T(8,128)(2,1)S(1)}, u32[]{:S(2)}, u32[]{:S(2)}) %collective-permute-start.4) | collective-permute-done | bytes 278560 | tf_op jit(solution)/shard_map/ppermute | solution.py:217
  25.0 1.9 %collective-permute-start.5 = (bf16[64,2176]{1,0:T(8,128)(2,1)S(1)}, bf16[64,2176]{1,0:T(8,128)(2,1)S(1)}, u32[]{:S(2)}, u32[]{:S(2)}) collective-permute-start(bf16[64,2176]{1,0:T(8,128)(2,1)S(1)} %collective-permute-done.4.refs_1_), channel_id=1, source_target_pairs={{0,5},{4,1},{5,8},{9,4},{8,13},{12,9},{13,14},{15,12},{14,11},{10,... | collective-permute-start | bytes 835592 | tf_op jit(solution)/shard_map/ppermute | solution.py:217
  26.9 1.4 %collective-permute-done.2.refs_0_ = bf16[64,2176]{1,0:T(8,128)(2,1)S(1)} collective-permute-done((bf16[64,2176]{1,0:T(8,128)(2,1)S(1)}, bf16[64,2176]{1,0:T(8,128)(2,1)S(1)}, u32[]{:S(2)}, u32[]{:S(2)}) %collective-permute-start.2) | collective-permute-done | bytes 278560 | tf_op jit(solution)/shard_map/ppermute | solution.py:215
  28.3 1.9 %collective-permute-start.6 = (bf16[64,2176]{1,0:T(8,128)(2,1)S(1)}, bf16[64,2176]{1,0:T(8,128)(2,1)S(1)}, u32[]{:S(2)}, u32[]{:S(2)}) collective-permute-start(bf16[64,2176]{1,0:T(8,128)(2,1)S(1)} %collective-permute-done.2.refs_0_), channel_id=1, source_target_pairs={{0,5},{4,1},{5,8},{9,4},{8,13},{12,9},{13,14},{15,12},{14,11},{10,... | collective-permute-start | bytes 835592 | tf_op jit(solution)/shard_map/ppermute | solution.py:215
  30.2 1.1 %collective-permute-done.5.refs_1_ = bf16[64,2176]{1,0:T(8,128)(2,1)S(1)} collective-permute-done((bf16[64,2176]{1,0:T(8,128)(2,1)S(1)}, bf16[64,2176]{1,0:T(8,128)(2,1)S(1)}, u32[]{:S(2)}, u32[]{:S(2)}) %collective-permute-start.5) | collective-permute-done | bytes 278560 | tf_op jit(solution)/shard_map/ppermute | solution.py:217
  31.3 3.3 %collective-permute-done.6.refs_2_ = bf16[64,2176]{1,0:T(8,128)(2,1)S(1)} collective-permute-done((bf16[64,2176]{1,0:T(8,128)(2,1)S(1)}, bf16[64,2176]{1,0:T(8,128)(2,1)S(1)}, u32[]{:S(2)}, u32[]{:S(2)}) %collective-permute-start.6) | collective-permute-done | bytes 278560 | tf_op jit(solution)/shard_map/ppermute | solution.py:215
  34.6 0.0 collective-permute-done.8.refs_6_.refs_3_.refs_4_
  34.6 0.0 collective-permute-done.7.refs_5_.refs_2_.refs_3_
  34.6 4.7 %expert.5 = (bf16[64,2048]{1,0:T(8,128)(2,1)S(1)}, bf16[64,2048]{1,0:T(8,128)(2,1)S(1)}, bf16[64,2048]{1,0:T(8,128)(2,1)S(1)}) custom-call(s32[2]{0:T(128)S(1)} %pad_add_fusion.first_ref, bf16[64,2176]{1,0:T(8,128)(2,1)S(1)} %collective-permute-done.2.refs_0_, bf16[64,2176]{1,0:T(8,128)(2,1)S(1)} %collective-permute-done.5.refs_1_, ...), custom_call_target="tpu_custom_call" | custom-call | tf_op jit(solution)/shard_map/expert/pallas_call | solution.py:155
  39.3 1.8 %collective-permute-start.9 = (bf16[64,2048]{1,0:T(8,128)(2,1)S(1)}, bf16[64,2048]{1,0:T(8,128)(2,1)S(1)}, u32[]{:S(2)}, u32[]{:S(2)}) collective-permute-start(bf16[64,2048]{1,0:T(8,128)(2,1)S(1)} %get-tuple-element.21), channel_id=1, source_target_pairs={{5,0},{1,4},{8,5},{4,9},{13,8},{9,12},{14,13},{12,15},{11,14},{15,... | collective-permute-start | bytes 786440 | tf_op jit(solution)/shard_map/ppermute | solution.py:235
  41.1 2.8 %expert.8 = (f32[64,2048]{1,0:T(8,128)S(1)}, f32[64,2048]{1,0:T(8,128)S(1)}, f32[64,2048]{1,0:T(8,128)S(1)}) custom-call(s32[2]{0:T(128)S(1)} %pad_add_fusion.first_ref, bf16[64,2176]{1,0:T(8,128)(2,1)S(1)} %pack.1.refs_0_, bf16[64,2176]{1,0:T(8,128)(2,1)S(1)} %collective-permute-done.refs_1_, bf16[64,2176]{1,0:T(8,128)(2,1)S(1)} %collective-permute-done.3.refs_2_, ...), custom_call_target="tpu_custom_call" | custom-call | tf_op jit(solution)/shard_map/expert/pallas_call | solution.py:155
  43.9 2.2 %expert.6 = (f32[64,2048]{1,0:T(8,128)S(1)}, f32[64,2048]{1,0:T(8,128)S(1)}) custom-call(s32[2]{0:T(128)S(1)} %pad_add_fusion.first_ref, bf16[64,2176]{1,0:T(8,128)(2,1)S(1)} %collective-permute-done.1.refs_0_, bf16[64,2176]{1,0:T(8,128)(2,1)S(1)} %collective-permute-done.4.refs_1_, bf16[2,2048,768]{2,1,0:T(8,128)(2,1)S(1)} %get-tuple-element.19.refs_3_.refs_2_, ...), custom_call_target="tpu_custom_call" | custom-call | tf_op jit(solution)/shard_map/expert/pallas_call | solution.py:155
  46.1 1.8 %collective-permute-start.13 = (bf16[64,2048]{1,0:T(8,128)(2,1)S(1)}, bf16[64,2048]{1,0:T(8,128)(2,1)S(1)}, u32[]{:S(2)}, u32[]{:S(2)}) collective-permute-start(bf16[64,2048]{1,0:T(8,128)(2,1)S(1)} %get-tuple-element.31), channel_id=1, source_target_pairs={{5,0},{1,4},{8,5},{4,9},{13,8},{9,12},{14,13},{12,15},{11,14},{15,... | collective-permute-start | bytes 786440 | tf_op jit(solution)/shard_map/ppermute | solution.py:238
  47.9 2.2 %expert.7 = (bf16[64,2048]{1,0:T(8,128)(2,1)S(1)}, bf16[64,2048]{1,0:T(8,128)(2,1)S(1)}) custom-call(s32[2]{0:T(128)S(1)} %pad_add_fusion.first_ref, bf16[64,2176]{1,0:T(8,128)(2,1)S(1)} %collective-permute-done.1.refs_0_, bf16[64,2176]{1,0:T(8,128)(2,1)S(1)} %collective-permute-done.4.refs_1_, ...), custom_call_target="tpu_custom_call" | custom-call | tf_op jit(solution)/shard_map/expert/pallas_call | solution.py:155
  50.1 2.8 %expert.9 = (bf16[64,2048]{1,0:T(8,128)(2,1)S(1)}, bf16[64,2048]{1,0:T(8,128)(2,1)S(1)}, bf16[64,2048]{1,0:T(8,128)(2,1)S(1)}) custom-call(s32[2]{0:T(128)S(1)} %pad_add_fusion.first_ref, bf16[64,2176]{1,0:T(8,128)(2,1)S(1)} %pack.1.refs_0_, bf16[64,2176]{1,0:T(8,128)(2,1)S(1)} %collective-permute-done.refs_1_, ...), custom_call_target="tpu_custom_call" | custom-call | tf_op jit(solution)/shard_map/expert/pallas_call | solution.py:155
  52.9 0.0 collective-permute-done.9
  52.9 0.1 add_convert_fusion.5
  53.0 1.8 %collective-permute-start.10 = (bf16[64,2048]{1,0:T(8,128)(2,1)S(1)}, bf16[64,2048]{1,0:T(8,128)(2,1)S(1)}, u32[]{:S(2)}, u32[]{:S(2)}) collective-permute-start(bf16[64,2048]{1,0:T(8,128)(2,1)S(1)} %add_convert_fusion.5), channel_id=1, source_target_pairs={{5,0},{1,4},{8,5},{4,9},{13,8},{9,12},{14,13},{12,15},{11,14},{15,... | collective-permute-start | bytes 786440 | tf_op jit(solution)/shard_map/ppermute | solution.py:235
  54.8 0.0 collective-permute-done.13
  54.8 0.1 add_convert_fusion.2
  54.9 0.0 copy-start.1
  54.9 0.0 copy-start.2
  54.9 0.3 collective-permute-start.14
  55.2 3.6 %collective-permute-done.10 = bf16[64,2048]{1,0:T(8,128)(2,1)S(1)} collective-permute-done((bf16[64,2048]{1,0:T(8,128)(2,1)S(1)}, bf16[64,2048]{1,0:T(8,128)(2,1)S(1)}, u32[]{:S(2)}, u32[]{:S(2)}) %collective-permute-start.10) | collective-permute-done | bytes 262176 | tf_op jit(solution)/shard_map/ppermute | solution.py:235
  58.8 0.1 add_convert_fusion.4
  58.9 2.1 %collective-permute-start.11 = (bf16[64,2048]{1,0:T(8,128)(2,1)S(1)}, bf16[64,2048]{1,0:T(8,128)(2,1)S(1)}, u32[]{:S(2)}, u32[]{:S(2)}) collective-permute-start(bf16[64,2048]{1,0:T(8,128)(2,1)S(1)} %add_convert_fusion.4), channel_id=1, source_target_pairs={{5,0},{1,4},{8,5},{4,9},{13,8},{9,12},{14,13},{12,15},{11,14},{15,... | collective-permute-start | bytes 786440 | tf_op jit(solution)/shard_map/ppermute | solution.py:235
  61.0 0.7 collective-permute-done.14
  61.6 0.1 add_convert_fusion.1
  61.7 0.1 collective-permute-start.15
  61.8 3.1 %collective-permute-done.11 = bf16[64,2048]{1,0:T(8,128)(2,1)S(1)} collective-permute-done((bf16[64,2048]{1,0:T(8,128)(2,1)S(1)}, bf16[64,2048]{1,0:T(8,128)(2,1)S(1)}, u32[]{:S(2)}, u32[]{:S(2)}) %collective-permute-start.11) | collective-permute-done | bytes 262176 | tf_op jit(solution)/shard_map/ppermute | solution.py:235
  64.9 0.1 add_convert_fusion.3
  65.0 2.0 %collective-permute-start.12 = (bf16[64,2048]{1,0:T(8,128)(2,1)S(1)}, bf16[64,2048]{1,0:T(8,128)(2,1)S(1)}, u32[]{:S(2)}, u32[]{:S(2)}) collective-permute-start(bf16[64,2048]{1,0:T(8,128)(2,1)S(1)} %add_convert_fusion.3), channel_id=1, source_target_pairs={{5,0},{1,4},{8,5},{4,9},{13,8},{9,12},{14,13},{12,15},{11,14},{15,... | collective-permute-start | bytes 786440 | tf_op jit(solution)/shard_map/ppermute | solution.py:241
  66.9 0.0 copy-done.1
  66.9 0.1 iota_compare_fusion
  67.0 0.0 copy-done
  67.0 0.0 copy-done.2
  67.0 0.7 fusion.22
  67.7 1.7 %fusion.17 = bf16[1,2,32,128]{3,2,1,0:T(8,128)(2,1)S(1)} fusion(bf16[2,640,4,128]{3,2,1,0:T(4,128)(2,1)} %param.20, f32[2,4,8,640]{3,2,1,0:T(8,128)S(1)} %get-tuple-element.37, f32[2,4,8]{2,1,0:T(4,128)S(1)} %get-tuple-element.36), kind=kOutput, calls=%fused_computation.11 | convolution fusion | flops 10575872 | bytes 1491200 | tf_op jit(solution)/shard_map/rkgl,rlkd->rkgd/dot_general | solution.py:31
  69.4 0.6 copy.31
  70.0 0.0 collective-permute-done.15
  70.0 0.8 %collective-permute-done.12 = bf16[64,2048]{1,0:T(8,128)(2,1)S(1)} collective-permute-done((bf16[64,2048]{1,0:T(8,128)(2,1)S(1)}, bf16[64,2048]{1,0:T(8,128)(2,1)S(1)}, u32[]{:S(2)}, u32[]{:S(2)}) %collective-permute-start.12) | collective-permute-done | bytes 262176 | tf_op jit(solution)/shard_map/ppermute | solution.py:241
  70.8 0.8 %add_convert_fusion = bf16[64,2048]{1,0:T(8,128)(2,1)} fusion(bf16[64,2048]{1,0:T(8,128)(2,1)S(1)} %get-tuple-element.34, bf16[64,2048]{1,0:T(8,128)(2,1)S(1)} %collective-permute-done.15, bf16[64,2048]{1,0:T(8,128)(2,1)S(1)} %collective-permute-done.12), kind=kLoop, calls=%fused_computation.12 | loop fusion | flops 786432 | bytes 1048576 | tf_op jit(solution)/shard_map/convert_element_type | solution.py:249
Async XLA Ops:
  0.6 66.4 %copy-start = (bf16[2,640,4,128]{3,2,1,0:T(4,128)(2,1)S(1)}, bf16[2,640,4,128]{3,2,1,0:T(4,128)(2,1)}, u32[]{:S(2)}) copy-start(bf16[2,640,4,128]{3,2,1,0:T(4,128)(2,1)} %param.19) | copy-start | bytes 3932164
  5.1 29.5 %collective-permute-start.7 = (bf16[2,2048,768]{2,1,0:T(8,128)(2,1)S(1)}, bf16[2,2048,768]{2,1,0:T(8,128)(2,1)S(1)}, u32[]{:S(2)}, u32[]{:S(2)}) collective-permute-start(bf16[2,2048,768]{2,1,0:T(8,128)(2,1)S(1)} %get-tuple-element.19.refs_3_.refs_2_), channel_id=1, source_target_pairs={{0,1},{1,0},{2,3},{3,2},{4,5},{5,4},{6,7},{7,6},{8,9},{9,8},{10,11... | collective-permute-start | bytes 18874376 | tf_op jit(solution)/shard_map/ppermute | solution.py:213
  5.6 28.9 %collective-permute-start.8 = (bf16[2,384,2048]{2,1,0:T(8,128)(2,1)S(1)}, bf16[2,384,2048]{2,1,0:T(8,128)(2,1)S(1)}, u32[]{:S(2)}, u32[]{:S(2)}) collective-permute-start(bf16[2,384,2048]{2,1,0:T(8,128)(2,1)S(1)} %get-tuple-element.20.refs_4_.refs_3_), channel_id=1, source_target_pairs={{0,1},{1,0},{2,3},{3,2},{4,5},{5,4},{6,7},{7,6},{8,9},{9,8},{10,11... | collective-permute-start | bytes 9437192 | tf_op jit(solution)/shard_map/ppermute | solution.py:213
  6.7 8.7 %collective-permute-start = (bf16[64,2176]{1,0:T(8,128)(2,1)S(1)}, bf16[64,2176]{1,0:T(8,128)(2,1)S(1)}, u32[]{:S(2)}, u32[]{:S(2)}) collective-permute-start(bf16[64,2176]{1,0:T(8,128)(2,1)S(1)} %pack.1.refs_0_), channel_id=1, source_target_pairs={{0,5},{4,1},{5,8},{9,4},{8,13},{12,9},{13,14},{15,12},{14,11},{10,... | collective-permute-start | bytes 835592 | tf_op jit(solution)/shard_map/ppermute | solution.py:208
  9.5 8.2 %collective-permute-start.3 = (bf16[64,2176]{1,0:T(8,128)(2,1)S(1)}, bf16[64,2176]{1,0:T(8,128)(2,1)S(1)}, u32[]{:S(2)}, u32[]{:S(2)}) collective-permute-start(bf16[64,2176]{1,0:T(8,128)(2,1)S(1)} %pack.1.refs_0_), channel_id=1, source_target_pairs={{1,5},{5,1},{4,8},{8,4},{9,13},{13,9},{12,14},{14,12},{15,11},{11,... | collective-permute-start | bytes 835592 | tf_op jit(solution)/shard_map/ppermute | solution.py:209
  15.5 6.5 %collective-permute-start.1 = (bf16[64,2176]{1,0:T(8,128)(2,1)S(1)}, bf16[64,2176]{1,0:T(8,128)(2,1)S(1)}, u32[]{:S(2)}, u32[]{:S(2)}) collective-permute-start(bf16[64,2176]{1,0:T(8,128)(2,1)S(1)} %collective-permute-done.refs_1_), channel_id=1, source_target_pairs={{0,5},{4,1},{5,8},{9,4},{8,13},{12,9},{13,14},{15,12},{14,11},{10,... | collective-permute-start | bytes 835592 | tf_op jit(solution)/shard_map/ppermute | solution.py:215
  17.7 7.3 %collective-permute-start.4 = (bf16[64,2176]{1,0:T(8,128)(2,1)S(1)}, bf16[64,2176]{1,0:T(8,128)(2,1)S(1)}, u32[]{:S(2)}, u32[]{:S(2)}) collective-permute-start(bf16[64,2176]{1,0:T(8,128)(2,1)S(1)} %collective-permute-done.3.refs_2_), channel_id=1, source_target_pairs={{0,5},{4,1},{5,8},{9,4},{8,13},{12,9},{13,14},{15,12},{14,11},{10,... | collective-permute-start | bytes 835592 | tf_op jit(solution)/shard_map/ppermute | solution.py:217
  22.0 6.3 %collective-permute-start.2 = (bf16[64,2176]{1,0:T(8,128)(2,1)S(1)}, bf16[64,2176]{1,0:T(8,128)(2,1)S(1)}, u32[]{:S(2)}, u32[]{:S(2)}) collective-permute-start(bf16[64,2176]{1,0:T(8,128)(2,1)S(1)} %collective-permute-done.1.refs_0_), channel_id=1, source_target_pairs={{0,5},{4,1},{5,8},{9,4},{8,13},{12,9},{13,14},{15,12},{14,11},{10,... | collective-permute-start | bytes 835592 | tf_op jit(solution)/shard_map/ppermute | solution.py:215
  25.0 6.3 %collective-permute-start.5 = (bf16[64,2176]{1,0:T(8,128)(2,1)S(1)}, bf16[64,2176]{1,0:T(8,128)(2,1)S(1)}, u32[]{:S(2)}, u32[]{:S(2)}) collective-permute-start(bf16[64,2176]{1,0:T(8,128)(2,1)S(1)} %collective-permute-done.4.refs_1_), channel_id=1, source_target_pairs={{0,5},{4,1},{5,8},{9,4},{8,13},{12,9},{13,14},{15,12},{14,11},{10,... | collective-permute-start | bytes 835592 | tf_op jit(solution)/shard_map/ppermute | solution.py:217
  28.3 6.3 %collective-permute-start.6 = (bf16[64,2176]{1,0:T(8,128)(2,1)S(1)}, bf16[64,2176]{1,0:T(8,128)(2,1)S(1)}, u32[]{:S(2)}, u32[]{:S(2)}) collective-permute-start(bf16[64,2176]{1,0:T(8,128)(2,1)S(1)} %collective-permute-done.2.refs_0_), channel_id=1, source_target_pairs={{0,5},{4,1},{5,8},{9,4},{8,13},{12,9},{13,14},{15,12},{14,11},{10,... | collective-permute-start | bytes 835592 | tf_op jit(solution)/shard_map/ppermute | solution.py:215
  39.3 13.6 %collective-permute-start.9 = (bf16[64,2048]{1,0:T(8,128)(2,1)S(1)}, bf16[64,2048]{1,0:T(8,128)(2,1)S(1)}, u32[]{:S(2)}, u32[]{:S(2)}) collective-permute-start(bf16[64,2048]{1,0:T(8,128)(2,1)S(1)} %get-tuple-element.21), channel_id=1, source_target_pairs={{5,0},{1,4},{8,5},{4,9},{13,8},{9,12},{14,13},{12,15},{11,14},{15,... | collective-permute-start | bytes 786440 | tf_op jit(solution)/shard_map/ppermute | solution.py:235
  46.1 8.7 %collective-permute-start.13 = (bf16[64,2048]{1,0:T(8,128)(2,1)S(1)}, bf16[64,2048]{1,0:T(8,128)(2,1)S(1)}, u32[]{:S(2)}, u32[]{:S(2)}) collective-permute-start(bf16[64,2048]{1,0:T(8,128)(2,1)S(1)} %get-tuple-element.31), channel_id=1, source_target_pairs={{5,0},{1,4},{8,5},{4,9},{13,8},{9,12},{14,13},{12,15},{11,14},{15,... | collective-permute-start | bytes 786440 | tf_op jit(solution)/shard_map/ppermute | solution.py:238
  53.0 5.8 %collective-permute-start.10 = (bf16[64,2048]{1,0:T(8,128)(2,1)S(1)}, bf16[64,2048]{1,0:T(8,128)(2,1)S(1)}, u32[]{:S(2)}, u32[]{:S(2)}) collective-permute-start(bf16[64,2048]{1,0:T(8,128)(2,1)S(1)} %add_convert_fusion.5), channel_id=1, source_target_pairs={{5,0},{1,4},{8,5},{4,9},{13,8},{9,12},{14,13},{12,15},{11,14},{15,... | collective-permute-start | bytes 786440 | tf_op jit(solution)/shard_map/ppermute | solution.py:235
  54.9 12.1 %copy-start.1 = (s32[2]{0:T(128)S(1)}, s32[2]{0:T(128)}, u32[]{:S(2)}) copy-start(s32[2]{0:T(128)} %param.21) | copy-start | bytes 28
  54.9 12.1 %copy-start.2 = (bf16[2,32,128]{2,1,0:T(8,128)(2,1)S(1)}, bf16[2,32,128]{2,1,0:T(8,128)(2,1)}, u32[]{:S(2)}) copy-start(bf16[2,32,128]{2,1,0:T(8,128)(2,1)} %param.18) | copy-start | bytes 49156
  54.9 6.8 %collective-permute-start.14 = (bf16[64,2048]{1,0:T(8,128)(2,1)S(1)}, bf16[64,2048]{1,0:T(8,128)(2,1)S(1)}, u32[]{:S(2)}, u32[]{:S(2)}) collective-permute-start(bf16[64,2048]{1,0:T(8,128)(2,1)S(1)} %add_convert_fusion.2), channel_id=1, source_target_pairs={{5,0},{1,4},{8,5},{4,9},{13,8},{9,12},{14,13},{12,15},{11,14},{15,... | collective-permute-start | bytes 786440 | tf_op jit(solution)/shard_map/ppermute | solution.py:238
  58.9 6.0 %collective-permute-start.11 = (bf16[64,2048]{1,0:T(8,128)(2,1)S(1)}, bf16[64,2048]{1,0:T(8,128)(2,1)S(1)}, u32[]{:S(2)}, u32[]{:S(2)}) collective-permute-start(bf16[64,2048]{1,0:T(8,128)(2,1)S(1)} %add_convert_fusion.4), channel_id=1, source_target_pairs={{5,0},{1,4},{8,5},{4,9},{13,8},{9,12},{14,13},{12,15},{11,14},{15,... | collective-permute-start | bytes 786440 | tf_op jit(solution)/shard_map/ppermute | solution.py:235
  61.7 8.3 %collective-permute-start.15 = (bf16[64,2048]{1,0:T(8,128)(2,1)S(1)}, bf16[64,2048]{1,0:T(8,128)(2,1)S(1)}, u32[]{:S(2)}, u32[]{:S(2)}) collective-permute-start(bf16[64,2048]{1,0:T(8,128)(2,1)S(1)} %add_convert_fusion.1), channel_id=1, source_target_pairs={{5,1},{1,5},{8,4},{4,8},{13,9},{9,13},{14,12},{12,14},{11,15},{15,... | collective-permute-start | bytes 786440 | tf_op jit(solution)/shard_map/ppermute | solution.py:242
  65.0 5.8 %collective-permute-start.12 = (bf16[64,2048]{1,0:T(8,128)(2,1)S(1)}, bf16[64,2048]{1,0:T(8,128)(2,1)S(1)}, u32[]{:S(2)}, u32[]{:S(2)}) collective-permute-start(bf16[64,2048]{1,0:T(8,128)(2,1)S(1)} %add_convert_fusion.3), channel_id=1, source_target_pairs={{5,0},{1,4},{8,5},{4,9},{13,8},{9,12},{14,13},{12,15},{11,14},{15,... | collective-permute-start | bytes 786440 | tf_op jit(solution)/shard_map/ppermute | solution.py:241
